TPU v7x, 32 devices: a whole 2x2x4 slice. The times are simulated.
32 devices in a mesh: row: 2 (over core), col: 16 (over z, y, x).
Axes of the slice: x: 2, y: 2, z: 4, core: 2. Of those that a mesh axis runs over, the one named last changes fastest.
Arguments:
- edge: bfloat16 [1024, 4096], P('row', 'col'), may hold values from -6 to 6
- double_layer: bfloat16 [4096, 8192], P(None, 'col'), may hold values from -0.25 to 0.25
- projector: bfloat16 [1024, 2048], P('row'), may hold values from -0.25 to 0.25
- charge_in: int32 [32], replicated, may hold values from 0 to 7
- charge_out: int32 [64], P('col'), may hold values from 0 to 7
- allowed: int32 [8, 8], replicated, may hold values from 0 to 1, as said below
- owner_slot_tile: int32 [16], replicated, may hold values from 0 to 15, each once
Outputs:
- contracted: bfloat16 [1024, 8192], P('row', 'col')
- corner: bfloat16 [2048, 8192], P('row', 'col')
Inputs may be any that keep to these rules, and one draw needn't show every extreme that they name: `owner_slot_tile`: each tile index appears once. Each charge has exactly one allowed partner charge, and every charge is the partner of exactly one charge.
All inputs are finite; a program needn't handle non-finite values.
Results may differ from a plain program's by a relative error of at most 0.005.
Values may be sent and summed in bfloat16 or wider, within the bound.
No kernel may reach another device: no remote copies, remote signals or barrier semaphores. Data moves between devices by JAX's collectives and lax.ppermute only.
A program may use at most 128 MiB of HBM per device.

v0:
```python
import jax
import jax.numpy as jnp
from jax import lax
from jax.sharding import PartitionSpec as P

TILE = 128


def block_mask(charge_in, charge_out, allowed):
    levels = jnp.arange(allowed.shape[0], dtype=jnp.int32)
    onehot_in = (charge_in[:, None] == levels[None, :]).astype(jnp.float32)
    onehot_out = (charge_out[:, None] == levels[None, :]).astype(jnp.float32)
    linked = jnp.dot(onehot_in, allowed.astype(jnp.float32), precision=lax.Precision.HIGHEST)
    linked = jnp.dot(linked, onehot_out.T, precision=lax.Precision.HIGHEST)
    return linked.astype(jnp.bfloat16)


def layer_under_mask(double_layer, blocks):
    incoming_tiles, out_tiles = blocks.shape
    shaped = double_layer.reshape(incoming_tiles, TILE, out_tiles, TILE)
    return (shaped * blocks[:, None, :, None]).reshape(incoming_tiles * TILE, out_tiles * TILE)


def owner_columns(owner_slot_tile):
    within_bounds = jnp.arange(TILE, dtype=jnp.int32)
    return (owner_slot_tile[:, None] * TILE + within_bounds[None, :]).reshape(-1)


def local(edge, double_layer, projector, charge_in, charge_out, allowed, owner_slot_tile):
    blocks = block_mask(charge_in, charge_out, allowed)
    masked_values = layer_under_mask(double_layer, blocks)
    contracted = jnp.dot(
        lax.all_gather(edge, "col", axis=1, tiled=True),
        masked_values,
        preferred_element_type=jnp.float32,
    ).astype(jnp.bfloat16)
    ordered = jnp.take(projector, owner_columns(owner_slot_tile), axis=1)
    corner = lax.psum_scatter(
        lax.dot_general(
            ordered, contracted, (((0,), (0,)), ((), ())), preferred_element_type=jnp.float32
        ),
        "row",
        scatter_dimension=0,
        tiled=True,
    )
    return (contracted, corner.astype(jnp.bfloat16))


def solution(mesh):
    return jax.shard_map(
        local,
        mesh=mesh,
        in_specs=(P("row", "col"), P(None, "col"), P("row", None), P(), P("col"), P(), P()),
        out_specs=(P("row", "col"), P("row", "col")),
        check_vma=False,
    )
```

profile of v0, /device:TPU:0, one launch (start us, length us, event | category | flops | bytes accessed | tf_op | source)
XLA Modules:
  0.0 130.1 jit_solution(4620089342191491523)
XLA Ops:
  7.2 0.0 copy-start.2
  7.2 0.0 all-gather.2.cloned.1.call-start
  7.2 0.7 all-gather.2.cloned.1.call-update
  7.9 0.0 reduce-scatter.2.cloned.1.call-start
  8.0 0.9 fusion.7
  8.9 0.8 convolution_convert_fusion
  9.7 0.1 copy.9
  9.8 2.9 %copy.10 = bf16[512,2048]{0,1:T(8,128)(2,1)S(1)} copy(bf16[512,2048]{1,0:T(8,128)(2,1)} %param.9) | data formatting | bytes 4194304 | tf_op args[2]
  12.7 0.0 copy-done.2
  12.7 0.1 iota_add_fusion
  12.8 9.2 %gather_fusion = bf16[2048,512]{1,0:T(8,128)(2,1)} fusion(bf16[512,2048]{0,1:T(8,128)(2,1)S(1)} %copy.10, s32[2048]{0:T(1024)S(1)} %broadcast_clamp_fusion), kind=kCustom, calls=%fused_computation | custom fusion | bytes 4202496 | tf_op jit(solution)/shard_map/jit(_take)/gather | solution.py:37
  22.0 0.1 compare_and_fusion
  22.1 78.1 %all-gather.2.cloned.1.call-done = bf16[512,4096]{1,0:T(8,128)(2,1)} async-done(((bf16[512,256]{1,0:T(8,128)(2,1)}), bf16[512,4096]{1,0:T(8,128)(2,1)}) %all-gather.2.cloned.1.call-update) | async-done | bytes 4194320 | tf_op jit(solution)/shard_map/all_gather | solution.py:33
  100.2 0.0 copy-start.1
  100.2 1.1 mul.15
  101.4 1.0 copy-done.1
  102.4 0.0 copy-start
  102.4 4.8 %fusion.5 = bf16[512,512]{1,0:T(8,128)(2,1)S(1)} fusion(bf16[512,4096]{1,0:T(8,128)(2,1)} %all-gather.2.cloned.1.call-done, bf16[4096,512]{1,0:T(8,128)(2,1)S(1)} %copy-done.1, bf16[512,8,4,128]{3,2,1,0:T(4,128)(2,1)S(1)} %bitcast.17), kind=kOutput, calls=%fused_computation.7 | convolution fusion | flops 2149842944 | bytes 13107200 | tf_op jit(solution)/shard_map/dot_general | solution.py:32
  107.3 0.0 copy-done
  107.3 2.9 %fusion.2 = f32[2048,512]{1,0:T(8,128)} fusion(bf16[512,512]{1,0:T(8,128)(2,1)S(1)} %fusion.5, bf16[2048,512]{1,0:T(8,128)(2,1)S(1)} %copy-done, pred[2048]{0:T(1024)(128)(4,1)S(1)} %compare_and_fusion), kind=kOutput, calls=%fused_computation.4 | convolution fusion | flops 1074790400 | bytes 6817792 | tf_op jit(solution)/shard_map/dot_general | solution.py:39
  110.2 0.0 reduce-scatter.2.cloned.1.call-update
  110.2 1.0 copy.11
  111.2 9.4 %reduce-scatter.2.cloned.1.call-done = f32[1024,512]{1,0:T(8,128)} async-done(((f32[2048,512]{1,0:T(8,128)}), f32[1024,512]{1,0:T(8,128)}) %reduce-scatter.2.cloned.1.call-update) | async-done | bytes 2097168 | tf_op jit(solution)/shard_map/reduce_scatter | solution.py:38
  120.6 2.7 %convert_element_type.21 = bf16[1024,512]{1,0:T(8,128)(2,1)} convert(f32[1024,512]{1,0:T(8,128)} %reduce-scatter.2.cloned.1.call-done) | non-fusion elementwise | flops 524288 | bytes 3145728 | tf_op jit(solution)/shard_map/convert_element_type | solution.py:46
  (3 shorter events, 0.0 us)
Async XLA Ops:
  7.2 5.5 %copy-start.2 = (s32[16]{0:T(128)S(1)}, s32[16]{0:T(128)}, u32[]{:S(2)}) copy-start(s32[16]{0:T(128)} %param.13) | copy-start | bytes 196
  7.2 93.1 %all-gather.2.cloned.1.call-start = ((), (), s32[]{:S(2)}) async-start(), calls=%async_computation.1 | async-start | bytes 4456448 | tf_op jit(solution)/shard_map/all_gather | solution.py:33
  7.9 112.7 %reduce-scatter.2.cloned.1.call-start = ((), (), s32[]{:S(2)}) async-start(), calls=%async_computation.2 | async-start | bytes 6291456 | tf_op jit(solution)/shard_map/reduce_scatter | solution.py:38
  100.2 2.2 %copy-start.1 = (bf16[4096,512]{1,0:T(8,128)(2,1)S(1)}, bf16[4096,512]{1,0:T(8,128)(2,1)}, u32[]{:S(2)}) copy-start(bf16[4096,512]{1,0:T(8,128)(2,1)} %param.8) | copy-start | bytes 12582916
  102.4 4.8 %copy-start = (bf16[2048,512]{1,0:T(8,128)(2,1)S(1)}, bf16[2048,512]{1,0:T(8,128)(2,1)}, u32[]{:S(2)}) copy-start(bf16[2048,512]{1,0:T(8,128)(2,1)} %gather_fusion) | copy-start | bytes 6291460
Sparse Core Ops, SparseCore 0:
  10.7 89.4 all-gather.1
  110.3 10.2 reduce-scatter.1
where the time goes:
time: 130 us
  waiting for transfers between devices  88.2 us (68%)
  local copies, waits for them, and re-layouts  15.4 us (12%)
  between operations  14.1 us (11%)
  matrix products  9.45 us (7%)
  other arithmetic  2.86 us (2%)
    all_gather x1, waiting for transfers between devices, local(): lax.all_gather(edge, 'col', axis=1, tiled=True)  78.1 us
    reduce_scatter x1, waiting for transfers between devices, local(): lax.psum_scatter(lax.dot_general(ordered, contracted, (((0,), (0,)), ((),...  9.37 us
    gather x1, local copies, waits for them, and re-layouts, local(): ordered = jnp.take(projector, owner_columns(owner_slot_tile), axis=1)  9.22 us
    unnamed x8, local copies, waits for them, and re-layouts  4.93 us
    dot_general x1, matrix products, local(): jnp.dot(lax.all_gather(edge, 'col', axis=1, tiled=True), masked_values, p...  4.84 us
    dot_general x1, matrix products, local(): lax.dot_general(ordered, contracted, (((0,), (0,)), ((), ())), preferred_...  2.88 us
    convert_element_type x1, other arithmetic, local(): return (contracted, corner.astype(jnp.bfloat16))  2.69 us
  transfers between devices with their start and end apart: 2, of which 2 were waited for; matrix products, arithmetic and copies ran while one was open for 12% of the time, Pallas kernels for 0%

commit v1 on v0

v1 whole, which is shorter than its diff:
```python
import functools

import jax
import jax.numpy as jnp
from jax import lax
from jax.experimental import pallas as pl
from jax.experimental.pallas import tpu as pltpu
from jax.sharding import PartitionSpec as P


TILE = 128

VMEM = pl.BlockSpec(memory_space=pltpu.VMEM)
SMEM = pl.BlockSpec(memory_space=pltpu.SMEM)
FAR = pl.BlockSpec(memory_space=pl.ANY)


def near(*arrays):
    return [pltpu.with_memory_space_constraint(a, pltpu.VMEM) for a in arrays]


def far(*arrays):
    return [pltpu.with_memory_space_constraint(a, pltpu.HBM) for a in arrays]


def grant(mebibytes):
    return pltpu.CompilerParams(vmem_limit_bytes=mebibytes << 20)


def mask_body(cin, cout, allowed, layer, out, met, sems):
    rows, columns = layer.shape
    tiles = columns // TILE
    for q in range(allowed.shape[0]):
        bits = jnp.int32(0)
        for c in range(tiles):
            bits = bits + jnp.where(allowed[q, cout[c]] != 0, 1 << c, 0)
        met[q] = bits

    def fetch(k):
        at = pl.ds(k * TILE, TILE)
        return pltpu.make_async_copy(layer.at[at, :], out.at[at, :], sems.at[k])

    for k in range(rows // TILE):
        pl.when(met[cin[k]] != 0)(lambda k=k: fetch(k).start())
    for k in range(rows // TILE):
        bits = met[cin[k]]

        @pl.when(bits == 0)
        def _():
            out[k * TILE:(k + 1) * TILE, :] = jnp.zeros((TILE, columns), out.dtype)

    for k in range(rows // TILE):
        bits = met[cin[k]]

        @pl.when(bits != 0)
        def _():
            fetch(k).wait()
            for c in range(tiles):

                @pl.when(lax.bitwise_and(bits, 1 << c) == 0)
                def _():
                    out[k * TILE:(k + 1) * TILE, c * TILE:(c + 1) * TILE] = jnp.zeros((TILE, TILE), out.dtype)


def mask(tables, layer):
    return pl.pallas_call(
        mask_body,
        out_shape=pltpu.VMEM(layer.shape, layer.dtype),
        in_specs=[SMEM] * 3 + [FAR],
        out_specs=VMEM,
        scratch_shapes=[
            pltpu.SMEM((tables[2].shape[0],), jnp.int32),
            pltpu.SemaphoreType.DMA((layer.shape[0] // TILE,)),
        ],
        compiler_params=grant(8),
        cost_estimate=pl.CostEstimate(flops=0, bytes_accessed=2 * layer.size, transcendentals=0),
        name="mask",
    )(*far(*tables, layer))


def absorb_body(planes, names, fresh, masked, *refs):
    count = len(names)
    edges, out = refs[:count], refs[-1]
    depth = edges[0].shape[1]
    row, col = lax.axis_index("row"), lax.axis_index("col")
    plane, spot = lax.div(col, 4), lax.rem(col, 4)
    first = 1 + lax.rem(row, 2)
    flips = {"own": 0, "first": first, "second": 3 - first, "both": 3}
    layers = []
    for slot, which in names:
        block = lax.rem(plane + (planes - slot), planes) * 4 + (spot ^ flips[which])
        layers.append(masked[pl.ds(pl.multiple_of(block * depth, depth), depth), :])
    wide = jnp.concatenate([e[...] for e in edges], axis=1)
    total = jnp.dot(wide, jnp.concatenate(layers, axis=0), preferred_element_type=jnp.float32)
    if not fresh:
        total = total + refs[count][...]
    out[...] = total.astype(out.dtype)


def absorb(planes, names, masked, blocks, total, last):
    count, (rows, depth), columns = len(blocks), blocks[0].shape, masked.shape[1]
    extra = () if total is None else (total,)
    return pl.pallas_call(
        functools.partial(absorb_body, planes, names, total is None),
        out_shape=pltpu.VMEM((rows, columns), jnp.bfloat16 if last else jnp.float32),
        in_specs=[VMEM] * (1 + count + len(extra)),
        out_specs=VMEM,
        compiler_params=grant(8),
        cost_estimate=pl.CostEstimate(
            flops=2 * count * rows * depth * columns, bytes_accessed=4 * count * depth * columns, transcendentals=0
        ),
        name="absorb",
    )(*near(masked, *blocks, *extra))


def order_body(groups, chunks, slots, projector, *refs):
    outs, held, sems = refs[:groups], refs[-2], refs[-1]
    share = slots.shape[0] // groups
    step = projector.shape[0] // chunks
    row = lax.axis_index("row")
    copies = []
    for i in range(chunks):
        at = pl.ds(i * step, step)
        copies.append(pltpu.make_async_copy(projector.at[at, :], held.at[at, :], sems.at[i]))
        copies[-1].start()
    for i in range(chunks):
        copies[i].wait()
        for k in range(groups):
            for t in range(share):
                tile = slots[lax.rem(row + k, groups) * share + t]
                at = pl.ds(pl.multiple_of(tile * TILE, TILE), TILE)
                outs[k][t * TILE:(t + 1) * TILE, i * step:(i + 1) * step] = held[i * step:(i + 1) * step, at].T


def order(groups, slots, projector):
    chunks = 4
    rows, share = projector.shape[0], slots.shape[0] // groups
    return pl.pallas_call(
        functools.partial(order_body, groups, chunks),
        out_shape=[pltpu.VMEM((share * TILE, rows), projector.dtype)] * groups,
        in_specs=[SMEM, FAR],
        out_specs=[VMEM] * groups,
        scratch_shapes=[pltpu.VMEM(projector.shape, projector.dtype), pltpu.SemaphoreType.DMA((chunks,))],
        compiler_params=grant(8),
        cost_estimate=pl.CostEstimate(flops=0, bytes_accessed=4 * projector.size, transcendentals=0),
        name="order",
    )(*far(slots, projector))


def own_corner_body(ordered, contracted, total, kept, sem):
    copy = pltpu.make_async_copy(contracted, kept, sem)
    copy.start()
    total[...] = jnp.dot(ordered[...], contracted[...], preferred_element_type=jnp.float32)
    copy.wait()


def own_corner(ordered, contracted):
    (rows, depth), columns = ordered.shape, contracted.shape[1]
    return pl.pallas_call(
        own_corner_body,
        out_shape=[
            pltpu.VMEM((rows, columns), jnp.float32),
            jax.ShapeDtypeStruct(contracted.shape, contracted.dtype),
        ],
        in_specs=[VMEM] * 2,
        out_specs=[VMEM, FAR],
        scratch_shapes=[pltpu.SemaphoreType.DMA],
        compiler_params=grant(8),
        cost_estimate=pl.CostEstimate(flops=2 * rows * depth * columns, bytes_accessed=contracted.size, transcendentals=0),
        name="own_corner",
    )(*near(ordered, contracted))


def corner_body(chunks, ordered, contracted, total, out, held, sems):
    step = ordered.shape[0] // chunks
    copies = []
    for i in range(chunks):
        at = pl.ds(i * step, step)
        term = jnp.dot(ordered[at, :], contracted[...], preferred_element_type=jnp.float32)
        held[at, :] = (total[at, :] + term).astype(held.dtype)
        copies.append(pltpu.make_async_copy(held.at[at, :], out.at[at, :], sems.at[i]))
        copies[-1].start()
    for copy in copies:
        copy.wait()


def corner_sum(ordered, contracted, total):
    chunks, kind = 4, jnp.bfloat16
    (rows, depth), columns = ordered.shape, contracted.shape[1]
    return pl.pallas_call(
        functools.partial(corner_body, chunks),
        out_shape=jax.ShapeDtypeStruct((rows, columns), kind),
        in_specs=[VMEM] * 3,
        out_specs=FAR,
        scratch_shapes=[pltpu.VMEM((rows, columns), kind), pltpu.SemaphoreType.DMA((chunks,))],
        compiler_params=grant(8),
        cost_estimate=pl.CostEstimate(flops=2 * rows * depth * columns, bytes_accessed=2 * rows * columns, transcendentals=0),
        name="corner",
    )(*near(ordered, contracted, total))


def more_corner_body(ordered, contracted, total, out):
    out[...] = total[...] + jnp.dot(ordered[...], contracted[...], preferred_element_type=jnp.float32)


def more_corner(ordered, contracted, total):
    return pl.pallas_call(
        more_corner_body,
        out_shape=pltpu.VMEM(total.shape, total.dtype),
        in_specs=[VMEM] * 3,
        out_specs=VMEM,
        compiler_params=grant(8),
        name="more_corner",
    )(*near(ordered, contracted, total))


def plan(planes):
    up = planes // 2
    four = ("own", "first", "second", "both")
    late = []
    for s in range(1, up + 1):
        late += [s] if s > 1 else []
        late += [planes - s] if s < planes - s else []
    steps = [("hop", 1), ("first", 0), ("second", 0), ("hop", planes - 1), ("order",), ("pass",)]
    steps += [("both", 0), ("second", 1), ("hop", 2)]
    for i, s in enumerate(late):
        steps += [("first", s)]
        if i > 0:
            steps += [("both", late[i - 1])]
        if 1 < s < up or s > up + 1:
            steps += [("hop", s + 1 if s < up else s - 1)]
        if i == 1:
            steps += [("relay", "both")]
        steps += [("second", s)]
        if i == 0:
            steps += [("mask",), ("relay", "first")]
        else:
            steps += [("absorb", late[i - 2] if i > 1 else 0, four)]
    last = late[-1]
    steps += [("both", last), ("absorb", 1, four[:1] + four[2:3])]
    steps += [("absorb", s, four) for s in late[-2:-1]]
    return steps + [("absorb", last, four[:3]), ("absorb", 1, four[1:2] + four[3:]), ("absorb", last, four[3:])]


def local(groups, n, edge, double_layer, projector, charge_in, charge_out, allowed, owner_slot_tile):
    planes = n // 4
    up = planes // 2
    got = {("own", 0): edge}
    total = None
    steps = plan(planes)

    def plane_shift(value, by):
        return lax.ppermute(value, "col", [(c, (c // 4 + by) % planes * 4 + c % 4) for c in range(n)])

    def across(value, which):
        flip = lambda r: which if r % 2 == 0 else 3 - which
        pairs = [(r * n + c, r * n + (c ^ flip(r))) for r in range(groups) for c in range(n)]
        return lax.ppermute(value, ("row", "col"), pairs)

    def row_shift(value, by):
        return lax.ppermute(value, "row", [(r, (r + by) % groups) for r in range(groups)])

    for step in steps:
        kind, s = step[0], step[-1 if len(step) < 3 else 1]
        if kind == "hop":
            before = s - 1 if s <= up else (s + 1) % planes
            got[("own", s)] = plane_shift(got[("own", before)], 1 if s <= up else -1)
        elif kind == "first":
            got[(kind, s)] = across(got[("own", s)], 1)
        elif kind == "second":
            got[(kind, s)] = across(got[("own", s)], 2)
        elif kind == "both":
            got[(kind, s)] = across(got[("first", s)], 2)
        elif kind == "relay":
            got[(s, 1)] = plane_shift(got[(s, 0)], 1)
        elif kind == "mask":
            masked = mask((charge_in, charge_out, allowed), double_layer)
        elif kind == "order":
            theirs = list(order(groups, owner_slot_tile, projector))
        elif kind == "pass":
            for k in range(1, groups):
                theirs[k] = row_shift(theirs[k], k)
        elif kind == "absorb":
            names = [(s, which) for which in step[2]]
            blocks = [got[(which, s)] for s, which in names]
            total = absorb(planes, names, masked, blocks, total, step == steps[-1])

    held = {}
    for k in range(1, groups):
        held[k] = row_shift(total, k)
    corner, contracted = own_corner(theirs[0], total)
    for k in range(1, groups - 1):
        corner = more_corner(theirs[k], held[k], corner)
    corner = corner_sum(theirs[groups - 1], held[groups - 1], corner)
    return contracted, corner


def solution(mesh):
    groups, n = mesh.shape["row"], mesh.shape["col"]

    def body(*arrays):
        return local(groups, n, *arrays)

    return jax.shard_map(
        body,
        mesh=mesh,
        in_specs=(P("row", "col"), P(None, "col"), P("row", None), P(), P("col"), P(), P()),
        out_specs=(P("row", "col"), P("row", "col")),
        check_vma=False,
    )
```

time: 130 us -> 52 us (0.40)
  waiting for transfers between devices: 88.2 us -> 20.5 us
  starting transfers between devices: 0.08 us -> 20.1 us
  local copies, waits for them, and re-layouts: 15.4 us -> 0.01 us
  between operations: 14.1 us -> 0.77 us
  Pallas kernels: 0 us -> 10.4 us
  matrix products: 9.45 us -> 0 us
  other arithmetic: 2.86 us -> 0 us
    all_gather x1 -> x0, waiting for transfers between devices: 78.1 us -> none  [local(): lax.all_gather(edge, 'col', axis=1, tiled=True)]
    ppermute x0 -> x17, waiting for transfers between devices: none -> 20.5 us  [the longest x5 14.9 us: plane_shift(): lax.ppermute(value, 'col', [(c, (c // 4 + by) % planes * 4 + c % 4) for c...]
    ppermute x0 -> x17, starting transfers between devices: none -> 20.1 us  [the longest x10 13.2 us: across(): return lax.ppermute(value, ('row', 'col'), pairs)]
    pallas_call x0 -> x10, Pallas kernels: none -> 10.4 us  [the longest x6 3.23 us: absorb(): pl.pallas_call(functools.partial(absorb_body, planes, names, total is Non...]
    dot_general x4 -> x0, matrix products: 9.45 us -> none  [the longest x1 4.84 us: local(): jnp.dot(lax.all_gather(edge, 'col', axis=1, tiled=True), masked_values, p...]
    reduce_scatter x1 -> x0, waiting for transfers between devices: 9.37 us -> none  [local(): lax.psum_scatter(lax.dot_general(ordered, contracted, (((0,), (0,)), ((),...]
    gather x1 -> x0, local copies, waits for them, and re-layouts: 9.22 us -> none  [local(): ordered = jnp.take(projector, owner_columns(owner_slot_tile), axis=1)]
    unnamed x8 -> x2, local copies, waits for them, and re-layouts: 4.93 us -> 0.01 us
  transfers between devices with their start and end apart: 2 -> 17, of which waited for: 2 -> 8; matrix products, arithmetic and copies ran while one was open for 12% -> 0% of each run, Pallas kernels for 0% -> 17%
where the time goes in v1:
time: 52 us; the launch traced here: 51.7 us
  waiting for transfers between devices  20.5 us (39%)
  starting transfers between devices  20.1 us (39%)
  Pallas kernels  10.4 us (20%)
  between operations  0.77 us (1%)
    ppermute x5, waiting for transfers between devices, plane_shift(): lax.ppermute(value, 'col', [(c, (c // 4 + by) % planes * 4 + c % 4) for c...  14.9 us
    ppermute x10, starting transfers between devices, across(): return lax.ppermute(value, ('row', 'col'), pairs)  13.2 us
    ppermute x5, starting transfers between devices, plane_shift(): lax.ppermute(value, 'col', [(c, (c // 4 + by) % planes * 4 + c % 4) for c...  6.76 us
    ppermute x10, waiting for transfers between devices, across(): return lax.ppermute(value, ('row', 'col'), pairs)  4.55 us
    pallas_call x6, Pallas kernels, absorb(): pl.pallas_call(functools.partial(absorb_body, planes, names, total is Non...  3.23 us
    pallas_call x1, Pallas kernels, order(): pl.pallas_call(functools.partial(order_body, groups, chunks), out_shape=[...  2.51 us
    pallas_call x1, Pallas kernels, mask(): pl.pallas_call(mask_body, out_shape=pltpu.VMEM(layer.shape, layer.dtype),...  2.42 us
    pallas_call x1, Pallas kernels, corner_sum(): pl.pallas_call(functools.partial(corner_body, chunks), out_shape=jax.Shap...  1.45 us
  transfers between devices with their start and end apart: 17, of which 8 were waited for; matrix products, arithmetic and copies ran while one was open for 0% of the time, Pallas kernels for 17%

profile of v1, /device:TPU:0, one launch (start us, length us, event | category | flops | bytes accessed | tf_op | source)
XLA Modules:
  0.0 51.7 jit_solution(11654036036262546164)
XLA Ops:
  0.6 5.1 %collective-permute-start.9 = (bf16[512,256]{1,0:T(8,128)(2,1)}, bf16[512,256]{1,0:T(8,128)(2,1)S(1)}, u32[]{:S(2)}, u32[]{:S(2)}) collective-permute-start(bf16[512,256]{1,0:T(8,128)(2,1)} %refs_0_.1), channel_id=1, source_target_pairs={{0,12},{1,13},{2,14},{3,15},{4,0},{5,1},{6,2},{7,3},{8,4},{9,5},{1... | collective-permute-start | bytes 786440 | tf_op jit(solution)/shard_map/ppermute | solution.py:253
  5.8 0.0 collective-permute-start
  5.8 1.5 %collective-permute-start.4 = (bf16[512,256]{1,0:T(8,128)(2,1)}, bf16[512,256]{1,0:T(8,128)(2,1)S(1)}, u32[]{:S(2)}, u32[]{:S(2)}) collective-permute-start(bf16[512,256]{1,0:T(8,128)(2,1)} %refs_0_.1), channel_id=1, source_target_pairs={{0,1},{1,0},{2,3},{3,2},{4,5},{5,4},{6,7},{7,6},{8,9},{9,8},{10,11... | collective-permute-start | bytes 786440 | tf_op jit(solution)/shard_map/ppermute | solution.py:258
  7.3 1.5 %collective-permute-start.14 = (bf16[512,256]{1,0:T(8,128)(2,1)}, bf16[512,256]{1,0:T(8,128)(2,1)S(1)}, u32[]{:S(2)}, u32[]{:S(2)}) collective-permute-start(bf16[512,256]{1,0:T(8,128)(2,1)} %refs_0_.1), channel_id=1, source_target_pairs={{0,2},{1,3},{2,0},{3,1},{4,6},{5,7},{6,4},{7,5},{8,10},{9,11},{10,... | collective-permute-start | bytes 786440 | tf_op jit(solution)/shard_map/ppermute | solution.py:258
  8.8 4.0 %collective-permute-done.9.refs_0_ = bf16[512,256]{1,0:T(8,128)(2,1)S(1)} collective-permute-done((bf16[512,256]{1,0:T(8,128)(2,1)}, bf16[512,256]{1,0:T(8,128)(2,1)S(1)}, u32[]{:S(2)}, u32[]{:S(2)}) %collective-permute-start.9) | collective-permute-done | bytes 262176 | tf_op jit(solution)/shard_map/ppermute | solution.py:253
  12.8 1.5 %collective-permute-start.10 = (bf16[512,256]{1,0:T(8,128)(2,1)S(1)}, bf16[512,256]{1,0:T(8,128)(2,1)S(1)}, u32[]{:S(2)}, u32[]{:S(2)}) collective-permute-start(bf16[512,256]{1,0:T(8,128)(2,1)S(1)} %collective-permute-done.9.refs_0_), channel_id=1, source_target_pairs={{0,1},{1,0},{2,3},{3,2},{4,5},{5,4},{6,7},{7,6},{8,9},{9,8},{10,11... | collective-permute-start | bytes 786440 | tf_op jit(solution)/shard_map/ppermute | solution.py:258
  14.3 3.8 %collective-permute-done.refs_0_ = bf16[512,256]{1,0:T(8,128)(2,1)S(1)} collective-permute-done((bf16[512,256]{1,0:T(8,128)(2,1)}, bf16[512,256]{1,0:T(8,128)(2,1)S(1)}, u32[]{:S(2)}, u32[]{:S(2)}) %collective-permute-start) | collective-permute-done | bytes 262176 | tf_op jit(solution)/shard_map/ppermute | solution.py:253
  18.1 1.6 %collective-permute-start.1 = (bf16[512,256]{1,0:T(8,128)(2,1)S(1)}, bf16[512,256]{1,0:T(8,128)(2,1)S(1)}, u32[]{:S(2)}, u32[]{:S(2)}) collective-permute-start(bf16[512,256]{1,0:T(8,128)(2,1)S(1)} %collective-permute-done.refs_0_), channel_id=1, source_target_pairs={{0,4},{1,5},{2,6},{3,7},{4,8},{5,9},{6,10},{7,11},{8,12},{9,13},{1... | collective-permute-start | bytes 786440 | tf_op jit(solution)/shard_map/ppermute | solution.py:253
  19.7 0.0 collective-permute-done.4.refs_1_
  19.7 1.5 %collective-permute-start.6 = (bf16[512,256]{1,0:T(8,128)(2,1)S(1)}, bf16[512,256]{1,0:T(8,128)(2,1)S(1)}, u32[]{:S(2)}, u32[]{:S(2)}) collective-permute-start(bf16[512,256]{1,0:T(8,128)(2,1)S(1)} %collective-permute-done.4.refs_1_), channel_id=1, source_target_pairs={{0,2},{1,3},{2,0},{3,1},{4,6},{5,7},{6,4},{7,5},{8,10},{9,11},{10,... | collective-permute-start | bytes 786440 | tf_op jit(solution)/shard_map/ppermute | solution.py:258
  21.2 0.5 collective-permute-start.13
  21.7 0.0 collective-permute-done.14.refs_2_
  21.7 1.5 %collective-permute-start.11 = (bf16[512,256]{1,0:T(8,128)(2,1)S(1)}, bf16[512,256]{1,0:T(8,128)(2,1)S(1)}, u32[]{:S(2)}, u32[]{:S(2)}) collective-permute-start(bf16[512,256]{1,0:T(8,128)(2,1)S(1)} %collective-permute-done.9.refs_0_), channel_id=1, source_target_pairs={{0,2},{1,3},{2,0},{3,1},{4,6},{5,7},{6,4},{7,5},{8,10},{9,11},{10,... | collective-permute-start | bytes 786440 | tf_op jit(solution)/shard_map/ppermute | solution.py:258
  23.2 0.0 collective-permute-done.10.refs_1_
  23.2 0.5 collective-permute-start.12
  23.7 3.3 %collective-permute-done.1.refs_0_ = bf16[512,256]{1,0:T(8,128)(2,1)S(1)} collective-permute-done((bf16[512,256]{1,0:T(8,128)(2,1)S(1)}, bf16[512,256]{1,0:T(8,128)(2,1)S(1)}, u32[]{:S(2)}, u32[]{:S(2)}) %collective-permute-start.1) | collective-permute-done | bytes 262176 | tf_op jit(solution)/shard_map/ppermute | solution.py:253
  27.0 1.5 %collective-permute-start.2 = (bf16[512,256]{1,0:T(8,128)(2,1)S(1)}, bf16[512,256]{1,0:T(8,128)(2,1)S(1)}, u32[]{:S(2)}, u32[]{:S(2)}) collective-permute-start(bf16[512,256]{1,0:T(8,128)(2,1)S(1)} %collective-permute-done.1.refs_0_), channel_id=1, source_target_pairs={{0,1},{1,0},{2,3},{3,2},{4,5},{5,4},{6,7},{7,6},{8,9},{9,8},{10,11... | collective-permute-start | bytes 786440 | tf_op jit(solution)/shard_map/ppermute | solution.py:258
  28.5 2.5 %order.1 = (bf16[1024,512]{1,0:T(8,128)(2,1)S(1)}, bf16[1024,512]{1,0:T(8,128)(2,1)S(1)}) custom-call(s32[16]{0:T(128)} %slots.1, bf16[512,2048]{1,0:T(8,128)(2,1)} %projector.1), custom_call_target="tpu_custom_call" | custom-call | bytes 4194304 | tf_op jit(solution)/shard_map/order/pallas_call | solution.py:138
  31.1 0.0 collective-permute-done.6.refs_3_
  31.1 0.0 copy-start
  31.1 0.1 collective-permute-start.15
  31.2 0.0 collective-permute-done.13.refs_1_
  31.2 1.6 %collective-permute-start.8 = (bf16[512,256]{1,0:T(8,128)(2,1)S(1)}, bf16[512,256]{1,0:T(8,128)(2,1)S(1)}, u32[]{:S(2)}, u32[]{:S(2)}) collective-permute-start(bf16[512,256]{1,0:T(8,128)(2,1)S(1)} %collective-permute-done.1.refs_0_), channel_id=1, source_target_pairs={{0,2},{1,3},{2,0},{3,1},{4,6},{5,7},{6,4},{7,5},{8,10},{9,11},{10,... | collective-permute-start | bytes 786440 | tf_op jit(solution)/shard_map/ppermute | solution.py:258
  32.8 1.7 %collective-permute-done.11.refs_2_ = bf16[512,256]{1,0:T(8,128)(2,1)S(1)} collective-permute-done((bf16[512,256]{1,0:T(8,128)(2,1)S(1)}, bf16[512,256]{1,0:T(8,128)(2,1)S(1)}, u32[]{:S(2)}, u32[]{:S(2)}) %collective-permute-start.11) | collective-permute-done | bytes 262176 | tf_op jit(solution)/shard_map/ppermute | solution.py:258
  34.5 0.0 collective-permute-start.5
  34.5 2.8 %collective-permute-done.12.refs_3_ = bf16[512,256]{1,0:T(8,128)(2,1)S(1)} collective-permute-done((bf16[512,256]{1,0:T(8,128)(2,1)S(1)}, bf16[512,256]{1,0:T(8,128)(2,1)S(1)}, u32[]{:S(2)}, u32[]{:S(2)}) %collective-permute-start.12) | collective-permute-done | bytes 262176 | tf_op jit(solution)/shard_map/ppermute | solution.py:258
  37.3 0.0 collective-permute-start.7
  37.3 0.0 collective-permute-done.2.refs_1_
  37.3 1.5 %collective-permute-start.3 = (bf16[512,256]{1,0:T(8,128)(2,1)S(1)}, bf16[512,256]{1,0:T(8,128)(2,1)S(1)}, u32[]{:S(2)}, u32[]{:S(2)}) collective-permute-start(bf16[512,256]{1,0:T(8,128)(2,1)S(1)} %collective-permute-done.2.refs_1_), channel_id=1, source_target_pairs={{0,2},{1,3},{2,0},{3,1},{4,6},{5,7},{6,4},{7,5},{8,10},{9,11},{10,... | collective-permute-start | bytes 786440 | tf_op jit(solution)/shard_map/ppermute | solution.py:258
  38.8 2.4 %mask.1.masked = bf16[4096,512]{1,0:T(8,128)(2,1)S(1)} custom-call(s32[32]{0:T(128)} %cin.1, s32[4]{0:T(128)} %cout.1, s32[8,8]{1,0:T(8,128)} %allowed.1, bf16[4096,512]{1,0:T(8,128)(2,1)} %layer.1), custom_call_target="tpu_custom_call" | custom-call | bytes 4194304 | tf_op jit(solution)/shard_map/mask/pallas_call | solution.py:66
  41.2 0.0 copy-done
  41.3 0.7 %absorb.6.refs_2_ = f32[512,512]{1,0:T(8,128)S(1)} custom-call(bf16[4096,512]{1,0:T(8,128)(2,1)S(1)} %mask.1.masked, bf16[512,256]{1,0:T(8,128)(2,1)S(1)} %copy-done, bf16[512,256]{1,0:T(8,128)(2,1)S(1)} %collective-permute-done.4.refs_1_, bf16[512,256]{1,0:T(8,128)(2,1)S(1)} %collective-permute-done.14.refs_2_, ...), custom_call_target="tpu_custom_call" | custom-call | flops 536870912 | bytes 2097152 | tf_op jit(solution)/shard_map/absorb/pallas_call | solution.py:103
  42.0 0.5 absorb.7.refs_4_
  42.4 0.7 %absorb.8.refs_3_ = f32[512,512]{1,0:T(8,128)S(1)} custom-call(bf16[4096,512]{1,0:T(8,128)(2,1)S(1)} %mask.1.masked, bf16[512,256]{1,0:T(8,128)(2,1)S(1)} %collective-permute-done.9.refs_0_, bf16[512,256]{1,0:T(8,128)(2,1)S(1)} %collective-permute-done.10.refs_1_, bf16[512,256]{1,0:T(8,128)(2,1)S(1)} %collective-permute-done.11.refs_2_, ...), custom_call_target="tpu_custom_call" | custom-call | flops 536870912 | bytes 2097152 | tf_op jit(solution)/shard_map/absorb/pallas_call | solution.py:103
  43.2 0.0 collective-permute-done.8.refs_2_
  43.2 0.6 %absorb.9.refs_2_ = f32[512,512]{1,0:T(8,128)S(1)} custom-call(bf16[4096,512]{1,0:T(8,128)(2,1)S(1)} %mask.1.masked, bf16[512,256]{1,0:T(8,128)(2,1)S(1)} %collective-permute-done.1.refs_0_, bf16[512,256]{1,0:T(8,128)(2,1)S(1)} %collective-permute-done.2.refs_1_, bf16[512,256]{1,0:T(8,128)(2,1)S(1)} %collective-permute-done.8.refs_2_, ...), custom_call_target="tpu_custom_call" | custom-call | flops 402653184 | bytes 1572864 | tf_op jit(solution)/shard_map/absorb/pallas_call | solution.py:103
  43.8 1.0 %collective-permute-done.5.refs_0_ = bf16[512,256]{1,0:T(8,128)(2,1)S(1)} collective-permute-done((bf16[512,256]{1,0:T(8,128)(2,1)S(1)}, bf16[512,256]{1,0:T(8,128)(2,1)S(1)}, u32[]{:S(2)}, u32[]{:S(2)}) %collective-permute-start.5) | collective-permute-done | bytes 262176 | tf_op jit(solution)/shard_map/ppermute | solution.py:253
  44.7 2.8 %collective-permute-done.7.refs_1_ = bf16[512,256]{1,0:T(8,128)(2,1)S(1)} collective-permute-done((bf16[512,256]{1,0:T(8,128)(2,1)S(1)}, bf16[512,256]{1,0:T(8,128)(2,1)S(1)}, u32[]{:S(2)}, u32[]{:S(2)}) %collective-permute-start.7) | collective-permute-done | bytes 262176 | tf_op jit(solution)/shard_map/ppermute | solution.py:253
  47.5 0.4 absorb.10.refs_1_
  48.0 0.0 collective-permute-done.3.refs_0_
  48.0 0.3 absorb.11.contracted
  48.3 0.1 collective-permute-start.16
  48.4 0.8 %own_corner.1 = (f32[1024,512]{1,0:T(8,128)S(1)}, bf16[512,512]{1,0:T(8,128)(2,1)}) custom-call(bf16[1024,512]{1,0:T(8,128)(2,1)S(1)} %get-tuple-element.6.ordered, bf16[512,512]{1,0:T(8,128)(2,1)S(1)} %absorb.11.contracted), custom_call_target="tpu_custom_call" | custom-call | flops 536870912 | bytes 262144 | tf_op jit(solution)/shard_map/own_corner/pallas_call | solution.py:159
  49.2 0.0 collective-permute-done.15.ordered
  49.2 1.1 %collective-permute-done.16.contracted = bf16[512,512]{1,0:T(8,128)(2,1)S(1)} collective-permute-done((bf16[512,512]{1,0:T(8,128)(2,1)S(1)}, bf16[512,512]{1,0:T(8,128)(2,1)S(1)}, u32[]{:S(2)}, u32[]{:S(2)}) %collective-permute-start.16) | collective-permute-done | bytes 524320 | tf_op jit(solution)/shard_map/ppermute | solution.py:261
  50.3 1.4 %corner.1 = bf16[1024,512]{1,0:T(8,128)(2,1)} custom-call(bf16[1024,512]{1,0:T(8,128)(2,1)S(1)} %collective-permute-done.15.ordered, bf16[512,512]{1,0:T(8,128)(2,1)S(1)} %collective-permute-done.16.contracted, f32[1024,512]{1,0:T(8,128)S(1)} %get-tuple-element.9.total), custom_call_target="tpu_custom_call" | custom-call | flops 536870912 | bytes 1048576 | tf_op jit(solution)/shard_map/corner/pallas_call | solution.py:190
Async XLA Ops:
  0.6 12.1 %collective-permute-start.9 = (bf16[512,256]{1,0:T(8,128)(2,1)}, bf16[512,256]{1,0:T(8,128)(2,1)S(1)}, u32[]{:S(2)}, u32[]{:S(2)}) collective-permute-start(bf16[512,256]{1,0:T(8,128)(2,1)} %refs_0_.1), channel_id=1, source_target_pairs={{0,12},{1,13},{2,14},{3,15},{4,0},{5,1},{6,2},{7,3},{8,4},{9,5},{1... | collective-permute-start | bytes 786440 | tf_op jit(solution)/shard_map/ppermute | solution.py:253
  5.8 12.3 %collective-permute-start = (bf16[512,256]{1,0:T(8,128)(2,1)}, bf16[512,256]{1,0:T(8,128)(2,1)S(1)}, u32[]{:S(2)}, u32[]{:S(2)}) collective-permute-start(bf16[512,256]{1,0:T(8,128)(2,1)} %refs_0_.1), channel_id=1, source_target_pairs={{0,4},{1,5},{2,6},{3,7},{4,8},{5,9},{6,10},{7,11},{8,12},{9,13},{1... | collective-permute-start | bytes 786440 | tf_op jit(solution)/shard_map/ppermute | solution.py:253
  5.8 13.9 %collective-permute-start.4 = (bf16[512,256]{1,0:T(8,128)(2,1)}, bf16[512,256]{1,0:T(8,128)(2,1)S(1)}, u32[]{:S(2)}, u32[]{:S(2)}) collective-permute-start(bf16[512,256]{1,0:T(8,128)(2,1)} %refs_0_.1), channel_id=1, source_target_pairs={{0,1},{1,0},{2,3},{3,2},{4,5},{5,4},{6,7},{7,6},{8,9},{9,8},{10,11... | collective-permute-start | bytes 786440 | tf_op jit(solution)/shard_map/ppermute | solution.py:258
  7.3 14.5 %collective-permute-start.14 = (bf16[512,256]{1,0:T(8,128)(2,1)}, bf16[512,256]{1,0:T(8,128)(2,1)S(1)}, u32[]{:S(2)}, u32[]{:S(2)}) collective-permute-start(bf16[512,256]{1,0:T(8,128)(2,1)} %refs_0_.1), channel_id=1, source_target_pairs={{0,2},{1,3},{2,0},{3,1},{4,6},{5,7},{6,4},{7,5},{8,10},{9,11},{10,... | collective-permute-start | bytes 786440 | tf_op jit(solution)/shard_map/ppermute | solution.py:258
  12.8 10.5 %collective-permute-start.10 = (bf16[512,256]{1,0:T(8,128)(2,1)S(1)}, bf16[512,256]{1,0:T(8,128)(2,1)S(1)}, u32[]{:S(2)}, u32[]{:S(2)}) collective-permute-start(bf16[512,256]{1,0:T(8,128)(2,1)S(1)} %collective-permute-done.9.refs_0_), channel_id=1, source_target_pairs={{0,1},{1,0},{2,3},{3,2},{4,5},{5,4},{6,7},{7,6},{8,9},{9,8},{10,11... | collective-permute-start | bytes 786440 | tf_op jit(solution)/shard_map/ppermute | solution.py:258
  18.1 9.0 %collective-permute-start.1 = (bf16[512,256]{1,0:T(8,128)(2,1)S(1)}, bf16[512,256]{1,0:T(8,128)(2,1)S(1)}, u32[]{:S(2)}, u32[]{:S(2)}) collective-permute-start(bf16[512,256]{1,0:T(8,128)(2,1)S(1)} %collective-permute-done.refs_0_), channel_id=1, source_target_pairs={{0,4},{1,5},{2,6},{3,7},{4,8},{5,9},{6,10},{7,11},{8,12},{9,13},{1... | collective-permute-start | bytes 786440 | tf_op jit(solution)/shard_map/ppermute | solution.py:253
  19.7 11.4 %collective-permute-start.6 = (bf16[512,256]{1,0:T(8,128)(2,1)S(1)}, bf16[512,256]{1,0:T(8,128)(2,1)S(1)}, u32[]{:S(2)}, u32[]{:S(2)}) collective-permute-start(bf16[512,256]{1,0:T(8,128)(2,1)S(1)} %collective-permute-done.4.refs_1_), channel_id=1, source_target_pairs={{0,2},{1,3},{2,0},{3,1},{4,6},{5,7},{6,4},{7,5},{8,10},{9,11},{10,... | collective-permute-start | bytes 786440 | tf_op jit(solution)/shard_map/ppermute | solution.py:258
  21.2 10.0 %collective-permute-start.13 = (bf16[512,256]{1,0:T(8,128)(2,1)S(1)}, bf16[512,256]{1,0:T(8,128)(2,1)S(1)}, u32[]{:S(2)}, u32[]{:S(2)}) collective-permute-start(bf16[512,256]{1,0:T(8,128)(2,1)S(1)} %collective-permute-done.refs_0_), channel_id=1, source_target_pairs={{0,2},{1,3},{2,0},{3,1},{4,6},{5,7},{6,4},{7,5},{8,10},{9,11},{10,... | collective-permute-start | bytes 786440 | tf_op jit(solution)/shard_map/ppermute | solution.py:258
  21.7 12.8 %collective-permute-start.11 = (bf16[512,256]{1,0:T(8,128)(2,1)S(1)}, bf16[512,256]{1,0:T(8,128)(2,1)S(1)}, u32[]{:S(2)}, u32[]{:S(2)}) collective-permute-start(bf16[512,256]{1,0:T(8,128)(2,1)S(1)} %collective-permute-done.9.refs_0_), channel_id=1, source_target_pairs={{0,2},{1,3},{2,0},{3,1},{4,6},{5,7},{6,4},{7,5},{8,10},{9,11},{10,... | collective-permute-start | bytes 786440 | tf_op jit(solution)/shard_map/ppermute | solution.py:258
  23.2 14.1 %collective-permute-start.12 = (bf16[512,256]{1,0:T(8,128)(2,1)S(1)}, bf16[512,256]{1,0:T(8,128)(2,1)S(1)}, u32[]{:S(2)}, u32[]{:S(2)}) collective-permute-start(bf16[512,256]{1,0:T(8,128)(2,1)S(1)} %collective-permute-done.10.refs_1_), channel_id=1, source_target_pairs={{0,2},{1,3},{2,0},{3,1},{4,6},{5,7},{6,4},{7,5},{8,10},{9,11},{10,... | collective-permute-start | bytes 786440 | tf_op jit(solution)/shard_map/ppermute | solution.py:258
  27.0 10.3 %collective-permute-start.2 = (bf16[512,256]{1,0:T(8,128)(2,1)S(1)}, bf16[512,256]{1,0:T(8,128)(2,1)S(1)}, u32[]{:S(2)}, u32[]{:S(2)}) collective-permute-start(bf16[512,256]{1,0:T(8,128)(2,1)S(1)} %collective-permute-done.1.refs_0_), channel_id=1, source_target_pairs={{0,1},{1,0},{2,3},{3,2},{4,5},{5,4},{6,7},{7,6},{8,9},{9,8},{10,11... | collective-permute-start | bytes 786440 | tf_op jit(solution)/shard_map/ppermute | solution.py:258
  31.1 10.2 %copy-start = (bf16[512,256]{1,0:T(8,128)(2,1)S(1)}, bf16[512,256]{1,0:T(8,128)(2,1)}, u32[]{:S(2)}) copy-start(bf16[512,256]{1,0:T(8,128)(2,1)} %refs_0_.1) | copy-start | bytes 786436
  31.1 18.1 %collective-permute-start.15 = (bf16[1024,512]{1,0:T(8,128)(2,1)S(1)}, bf16[1024,512]{1,0:T(8,128)(2,1)S(1)}, u32[]{:S(2)}, u32[]{:S(2)}) collective-permute-start(bf16[1024,512]{1,0:T(8,128)(2,1)S(1)} %get-tuple-element.8), channel_id=1, source_target_pairs={{0,16},{16,0},{1,17},{17,1},{2,18},{18,2},{3,19},{19,3},{4,20},{20... | collective-permute-start | bytes 3145736 | tf_op jit(solution)/shard_map/ppermute | solution.py:261
  31.2 12.0 %collective-permute-start.8 = (bf16[512,256]{1,0:T(8,128)(2,1)S(1)}, bf16[512,256]{1,0:T(8,128)(2,1)S(1)}, u32[]{:S(2)}, u32[]{:S(2)}) collective-permute-start(bf16[512,256]{1,0:T(8,128)(2,1)S(1)} %collective-permute-done.1.refs_0_), channel_id=1, source_target_pairs={{0,2},{1,3},{2,0},{3,1},{4,6},{5,7},{6,4},{7,5},{8,10},{9,11},{10,... | collective-permute-start | bytes 786440 | tf_op jit(solution)/shard_map/ppermute | solution.py:258
  34.5 10.3 %collective-permute-start.5 = (bf16[512,256]{1,0:T(8,128)(2,1)S(1)}, bf16[512,256]{1,0:T(8,128)(2,1)S(1)}, u32[]{:S(2)}, u32[]{:S(2)}) collective-permute-start(bf16[512,256]{1,0:T(8,128)(2,1)S(1)} %collective-permute-done.4.refs_1_), channel_id=1, source_target_pairs={{0,4},{1,5},{2,6},{3,7},{4,8},{5,9},{6,10},{7,11},{8,12},{9,13},{1... | collective-permute-start | bytes 786440 | tf_op jit(solution)/shard_map/ppermute | solution.py:253
  37.3 10.3 %collective-permute-start.7 = (bf16[512,256]{1,0:T(8,128)(2,1)S(1)}, bf16[512,256]{1,0:T(8,128)(2,1)S(1)}, u32[]{:S(2)}, u32[]{:S(2)}) collective-permute-start(bf16[512,256]{1,0:T(8,128)(2,1)S(1)} %collective-permute-done.6.refs_3_), channel_id=1, source_target_pairs={{0,4},{1,5},{2,6},{3,7},{4,8},{5,9},{6,10},{7,11},{8,12},{9,13},{1... | collective-permute-start | bytes 786440 | tf_op jit(solution)/shard_map/ppermute | solution.py:253
  37.3 10.7 %collective-permute-start.3 = (bf16[512,256]{1,0:T(8,128)(2,1)S(1)}, bf16[512,256]{1,0:T(8,128)(2,1)S(1)}, u32[]{:S(2)}, u32[]{:S(2)}) collective-permute-start(bf16[512,256]{1,0:T(8,128)(2,1)S(1)} %collective-permute-done.2.refs_1_), channel_id=1, source_target_pairs={{0,2},{1,3},{2,0},{3,1},{4,6},{5,7},{6,4},{7,5},{8,10},{9,11},{10,... | collective-permute-start | bytes 786440 | tf_op jit(solution)/shard_map/ppermute | solution.py:258
  48.3 2.0 %collective-permute-start.16 = (bf16[512,512]{1,0:T(8,128)(2,1)S(1)}, bf16[512,512]{1,0:T(8,128)(2,1)S(1)}, u32[]{:S(2)}, u32[]{:S(2)}) collective-permute-start(bf16[512,512]{1,0:T(8,128)(2,1)S(1)} %absorb.11.contracted), channel_id=1, source_target_pairs={{0,16},{16,0},{1,17},{17,1},{2,18},{18,2},{3,19},{19,3},{4,20},{20... | collective-permute-start | bytes 1572872 | tf_op jit(solution)/shard_map/ppermute | solution.py:261

commit v2 on v1

v2 whole, which is shorter than its diff:
```python
import functools

import jax
import jax.numpy as jnp
from jax import lax
from jax.experimental import pallas as pl
from jax.experimental.pallas import tpu as pltpu
from jax.sharding import PartitionSpec as P


TILE = 128
PIECES = 2

VMEM = pl.BlockSpec(memory_space=pltpu.VMEM)
SMEM = pl.BlockSpec(memory_space=pltpu.SMEM)
FAR = pl.BlockSpec(memory_space=pl.ANY)


def near(*arrays):
    return [pltpu.with_memory_space_constraint(a, pltpu.VMEM) for a in arrays]


def far(*arrays):
    return [pltpu.with_memory_space_constraint(a, pltpu.HBM) for a in arrays]


def grant(mebibytes):
    return pltpu.CompilerParams(vmem_limit_bytes=mebibytes << 20)


def prepare_body(groups, chunks, cin, cout, allowed, slots, layer, projector, masked, *refs):
    outs, (held, met, layer_sems, sems) = refs[:groups], refs[groups:]
    rows, columns = layer.shape
    tiles = columns // TILE
    step = projector.shape[0] // chunks
    share = slots.shape[0] // groups
    row = lax.axis_index("row")

    def part(i):
        at = pl.ds(i * step, step)
        return pltpu.make_async_copy(projector.at[at, :], held.at[at, :], sems.at[i])

    def fetch(k):
        at = pl.ds(k * TILE, TILE)
        return pltpu.make_async_copy(layer.at[at, :], masked.at[at, :], layer_sems.at[k])

    for i in range(chunks):
        part(i).start()
    for q in range(allowed.shape[0]):
        bits = jnp.int32(0)
        for c in range(tiles):
            bits = bits + jnp.where(allowed[q, cout[c]] != 0, 1 << c, 0)
        met[q] = bits
    for k in range(rows // TILE):
        pl.when(met[cin[k]] != 0)(lambda k=k: fetch(k).start())
    for i in range(chunks):
        part(i).wait()
        for k in range(groups):
            for t in range(share):
                tile = slots[lax.rem(row + k, groups) * share + t]
                at = pl.ds(pl.multiple_of(tile * TILE, TILE), TILE)
                outs[k][t * TILE:(t + 1) * TILE, i * step:(i + 1) * step] = held[i * step:(i + 1) * step, at].T
    for k in range(rows // TILE):
        bits = met[cin[k]]

        @pl.when(bits == 0)
        def _():
            masked[k * TILE:(k + 1) * TILE, :] = jnp.zeros((TILE, columns), masked.dtype)

        @pl.when(bits != 0)
        def _():
            fetch(k).wait()
            for c in range(tiles):

                @pl.when(lax.bitwise_and(bits, 1 << c) == 0)
                def _():
                    masked[k * TILE:(k + 1) * TILE, c * TILE:(c + 1) * TILE] = jnp.zeros((TILE, TILE), masked.dtype)


def prepare(groups, tables, slots, layer, projector):
    chunks = 4
    rows, share = projector.shape[0], slots.shape[0] // groups
    masked, *ordered = pl.pallas_call(
        functools.partial(prepare_body, groups, chunks),
        out_shape=[pltpu.VMEM(layer.shape, layer.dtype)]
        + [pltpu.VMEM((share * TILE, rows), projector.dtype)] * groups,
        in_specs=[SMEM] * 4 + [FAR] * 2,
        out_specs=[VMEM] * (1 + groups),
        scratch_shapes=[
            pltpu.VMEM(projector.shape, projector.dtype),
            pltpu.SMEM((tables[2].shape[0],), jnp.int32),
            pltpu.SemaphoreType.DMA((layer.shape[0] // TILE,)),
            pltpu.SemaphoreType.DMA((chunks,)),
        ],
        compiler_params=grant(8),
        cost_estimate=pl.CostEstimate(flops=0, bytes_accessed=2 * layer.size + 4 * projector.size, transcendentals=0),
        name="prepare",
    )(*far(*tables, slots, layer, projector))
    return masked, ordered


def absorb_body(planes, names, fresh, at, masked, *refs):
    count = len(names)
    edges, out = refs[:count], refs[-1]
    depth = edges[0].shape[1]
    row, col = lax.axis_index("row"), lax.axis_index("col")
    plane, spot = lax.div(col, 4), lax.rem(col, 4)
    first = 1 + lax.rem(row, 2)
    flips = {"own": 0, "first": first, "second": 3 - first, "both": 3}
    layers = []
    for slot, which in names:
        block = lax.rem(plane + (planes - slot), planes) * 4 + (spot ^ flips[which])
        layers.append(masked[pl.ds(pl.multiple_of(block * depth, depth), depth), :])
    wide = jnp.concatenate([e[...] for e in edges], axis=1)
    total = jnp.dot(wide, jnp.concatenate(layers, axis=0), preferred_element_type=jnp.float32)
    if not fresh:
        total = total + refs[count][at:at + wide.shape[0], :]
    out[...] = total.astype(out.dtype)


def absorb(planes, names, masked, blocks, total, at=0, last=False):
    count, (rows, depth), columns = len(blocks), blocks[0].shape, masked.shape[1]
    extra = () if total is None else (total,)
    return pl.pallas_call(
        functools.partial(absorb_body, planes, names, total is None, at),
        out_shape=pltpu.VMEM((rows, columns), jnp.bfloat16 if last else jnp.float32),
        in_specs=[VMEM] * (1 + count + len(extra)),
        out_specs=VMEM,
        compiler_params=grant(8),
        cost_estimate=pl.CostEstimate(
            flops=2 * count * rows * depth * columns, bytes_accessed=4 * count * depth * columns, transcendentals=0
        ),
        name="absorb",
    )(*near(masked, *blocks, *extra))


def corner_term_body(start, fresh, writes, ordered, contracted, *refs):
    depth, sems = contracted.shape[0], refs[-1]
    refs, copies = list(refs), []
    total = None if fresh else refs.pop(0)
    pieces = [refs.pop(0) for _ in range(writes)]
    for i, piece in enumerate(pieces):
        at = pl.ds(i * piece.shape[0], piece.shape[0])
        copies.append(pltpu.make_async_copy(piece, refs[1].at[at, :], sems.at[i]))
        copies[-1].start()
    term = jnp.dot(ordered[:, start:start + depth], contracted[...], preferred_element_type=jnp.float32)
    refs[0][...] = term if fresh else total[...] + term
    for copy in copies:
        copy.wait()


def corner_term(start, ordered, contracted, total=None, pieces=()):
    (depth, columns), count = contracted.shape, len(pieces)
    shapes, specs = [pltpu.VMEM((ordered.shape[0], columns), jnp.float32)], [VMEM]
    if pieces:
        shapes += [jax.ShapeDtypeStruct((count * depth, columns), contracted.dtype)]
        specs += [FAR]
    more = (() if total is None else (total,)) + tuple(pieces)
    return pl.pallas_call(
        functools.partial(corner_term_body, start, total is None, count),
        out_shape=shapes,
        in_specs=[VMEM] * (2 + len(more)),
        out_specs=specs,
        scratch_shapes=[pltpu.SemaphoreType.DMA((max(count, 1),))],
        compiler_params=grant(8),
        cost_estimate=pl.CostEstimate(
            flops=2 * ordered.shape[0] * contracted.size, bytes_accessed=2 * contracted.size, transcendentals=0
        ),
        name="corner_term",
    )(*near(ordered, contracted, *more))


def corner_body(start, chunks, ordered, contracted, total, out, held, sems):
    step, depth = ordered.shape[0] // chunks, contracted.shape[0]
    copies = []
    for i in range(chunks):
        at = pl.ds(i * step, step)
        term = jnp.dot(ordered[at, start:start + depth], contracted[...], preferred_element_type=jnp.float32)
        held[at, :] = (total[at, :] + term).astype(held.dtype)
        copies.append(pltpu.make_async_copy(held.at[at, :], out.at[at, :], sems.at[i]))
        copies[-1].start()
    for copy in copies:
        copy.wait()


def corner_sum(start, ordered, contracted, total):
    chunks, kind = 8, jnp.bfloat16
    rows, columns = total.shape
    return pl.pallas_call(
        functools.partial(corner_body, start, chunks),
        out_shape=jax.ShapeDtypeStruct((rows, columns), kind),
        in_specs=[VMEM] * 3,
        out_specs=FAR,
        scratch_shapes=[pltpu.VMEM((rows, columns), kind), pltpu.SemaphoreType.DMA((chunks,))],
        compiler_params=grant(8),
        cost_estimate=pl.CostEstimate(
            flops=2 * ordered.shape[0] * contracted.size, bytes_accessed=2 * rows * columns, transcendentals=0
        ),
        name="corner",
    )(*near(ordered, contracted, total))


def plan(planes):
    up = planes // 2
    whole = lambda s: tuple((s, kind) for kind in ("own", "first", "second", "both"))
    late = []
    for s in range(1, up + 1):
        late += [s] if s > 1 else []
        late += [planes - s] if s < planes - s else []
    steps = [("hop", 1), ("first", 0), ("second", 0), ("hop", planes - 1), ("prepare",)]
    steps += [("both", 0), ("hop", 2), ("second", 1)]
    for i, s in enumerate(late):
        steps += [("first", s)]
        hop = [("hop", s + 1 if s < up else s - 1)] if 1 < s < up or s > up + 1 else []
        if i == 0:
            steps += hop + [("pass",), ("relay", "first"), ("second", s)]
            continue
        if i == 1:
            steps += [("absorb", 0, whole(0) + ((1, "own"), (1, "second")))]
        else:
            steps += [("absorb", late[i - 2], whole(late[i - 2]))]
        steps += [("both", late[i - 1]), ("second", s)] + hop
        if i == 1:
            steps += [("relay", "both")]
    last = late[-1]
    steps += [("both", last)] + [("absorb", s, whole(s)) for s in late[-2:-1]]
    return steps + [("absorb", last, ((last, "own"), (last, "second"), (1, "first"), (1, "both")))]


def last_slot(planes):
    return next(step[1] for step in reversed(plan(planes)) if step[0] == "both")


def local(groups, n, edge, double_layer, projector, charge_in, charge_out, allowed, owner_slot_tile):
    planes = n // 4
    up = planes // 2
    last, height = last_slot(planes), edge.shape[0] // PIECES
    got = {("own", 0): edge}
    total = None
    steps = plan(planes)

    def plane_shift(value, by):
        return lax.ppermute(value, "col", [(c, (c // 4 + by) % planes * 4 + c % 4) for c in range(n)])

    def across(value, which):
        flip = lambda r: which if r % 2 == 0 else 3 - which
        pairs = [(r * n + c, r * n + (c ^ flip(r))) for r in range(groups) for c in range(n)]
        return lax.ppermute(value, ("row", "col"), pairs)

    def row_shift(value, by):
        return lax.ppermute(value, "row", [(r, (r + by) % groups) for r in range(groups)])

    for step in steps:
        kind, s = step[0], step[-1 if len(step) < 3 else 1]
        if kind == "hop":
            before = s - 1 if s <= up else (s + 1) % planes
            got[("own", s)] = plane_shift(got[("own", before)], 1 if s <= up else -1)
        elif s == last and kind in ("first", "both"):
            for i in range(PIECES):
                if kind == "first":
                    piece = across(got[("own", s)][i * height:(i + 1) * height], 1)
                else:
                    piece = across(got[("firsts", i)], 2)
                got[(kind + "s", i)] = piece
        elif kind == "first":
            got[(kind, s)] = across(got[("own", s)], 1)
        elif kind == "second":
            got[(kind, s)] = across(got[("own", s)], 2)
        elif kind == "both":
            got[(kind, s)] = across(got[("first", s)], 2)
        elif kind == "relay":
            got[(s, 1)] = plane_shift(got[(s, 0)], 1)
        elif kind == "prepare":
            tables = (charge_in, charge_out, allowed)
            masked, theirs = prepare(groups, tables, owner_slot_tile, double_layer, projector)
        elif kind == "pass":
            for k in range(1, groups):
                theirs[k] = row_shift(theirs[k], k)
        elif kind == "absorb":
            names = step[2]
            blocks = [got[(which, slot)] for slot, which in names]
            total = absorb(planes, names, masked, blocks, total)

    names = [(last, "first"), (last, "both")]
    pieces, held, corner = [], [], None
    for i in range(PIECES):
        blocks = [got[("firsts", i)], got[("boths", i)]]
        pieces.append(absorb(planes, names, masked, blocks, total, i * height, True))
        for k in range(1, groups):
            held.append((k, i * height, row_shift(pieces[i], k)))
        out = corner_term(i * height, theirs[0], pieces[i], corner, pieces if i == PIECES - 1 else ())
        corner = out[0]
    contracted = out[1]
    for k, start, piece in held[:-1]:
        corner = corner_term(start, theirs[k], piece, corner)[0]
    k, start, piece = held[-1]
    corner = corner_sum(start, theirs[k], piece, corner)
    return contracted, corner


def solution(mesh):
    groups, n = mesh.shape["row"], mesh.shape["col"]

    def body(*arrays):
        return local(groups, n, *arrays)

    return jax.shard_map(
        body,
        mesh=mesh,
        in_specs=(P("row", "col"), P(None, "col"), P("row", None), P(), P("col"), P(), P()),
        out_specs=(P("row", "col"), P("row", "col")),
        check_vma=False,
    )
```

time: 52 us -> 53.1 us (1.021)
  starting transfers between devices: 20.1 us -> 27.7 us
  waiting for transfers between devices: 20.5 us -> 14.4 us
    ppermute x5, waiting for transfers between devices: 14.9 us -> 4.54 us  [plane_shift(): lax.ppermute(value, 'col', [(c, (c // 4 + by) % planes * 4 + c % 4) for c...]
    ppermute x10 -> x12, waiting for transfers between devices: 4.55 us -> 9.81 us  [across(): return lax.ppermute(value, ('row', 'col'), pairs)]
    ppermute x5, starting transfers between devices: 6.76 us -> 10.9 us  [plane_shift(): lax.ppermute(value, 'col', [(c, (c // 4 + by) % planes * 4 + c % 4) for c...]
    ppermute x10 -> x12, starting transfers between devices: 13.2 us -> 16.6 us  [across(): return lax.ppermute(value, ('row', 'col'), pairs)]
    ppermute x2 -> x3, waiting for transfers between devices: 1.06 us -> 0.01 us  [row_shift(): lax.ppermute(value, 'row', [(r, (r + by) % groups) for r in range(groups)])]
    pallas_call x6 -> x5, Pallas kernels: 3.23 us -> 3.01 us  [absorb(): pl.pallas_call(functools.partial(absorb_body, planes, names, total is Non...]
    pallas_call x4 -> x5, Pallas kernels: 7.21 us -> 7.07 us  [the longest x1 4.13 us: prepare(): pl.pallas_call(functools.partial(prepare_body, groups, chunks), out_shape...]
  transfers between devices with their start and end apart: 17 -> 20, of which waited for: 8 -> 9; matrix products, arithmetic and copies ran while one was open for 0% -> 0% of each run, Pallas kernels for 17% -> 17%
where the time goes in v2:
time: 53.1 us; the launch traced here: 53 us
  starting transfers between devices  27.7 us (52%)
  waiting for transfers between devices  14.4 us (27%)
  Pallas kernels  10.1 us (19%)
  between operations  0.8 us (2%)
    ppermute x12, starting transfers between devices, across(): return lax.ppermute(value, ('row', 'col'), pairs)  16.6 us
    ppermute x5, starting transfers between devices, plane_shift(): lax.ppermute(value, 'col', [(c, (c // 4 + by) % planes * 4 + c % 4) for c...  10.9 us
    ppermute x12, waiting for transfers between devices, across(): return lax.ppermute(value, ('row', 'col'), pairs)  9.81 us
    ppermute x5, waiting for transfers between devices, plane_shift(): lax.ppermute(value, 'col', [(c, (c // 4 + by) % planes * 4 + c % 4) for c...  4.54 us
    pallas_call x1, Pallas kernels, prepare(): pl.pallas_call(functools.partial(prepare_body, groups, chunks), out_shape...  4.13 us
    pallas_call x5, Pallas kernels, absorb(): pl.pallas_call(functools.partial(absorb_body, planes, names, total is Non...  3.01 us
    pallas_call x3, Pallas kernels, corner_term(): pl.pallas_call(functools.partial(corner_term_body, start, total is None,...  1.71 us
    pallas_call x1, Pallas kernels, corner_sum(): pl.pallas_call(functools.partial(corner_body, start, chunks), out_shape=j...  1.23 us
  transfers between devices with their start and end apart: 20, of which 9 were waited for; matrix products, arithmetic and copies ran while one was open for 0% of the time, Pallas kernels for 17%

profile of v2, /device:TPU:0, one launch (start us, length us, event | category | flops | bytes accessed | tf_op | source)
XLA Modules:
  0.0 53.0 jit_solution(10335688422768613689)
XLA Ops:
  0.6 3.0 %collective-permute-start.5 = (bf16[512,256]{1,0:T(8,128)(2,1)}, bf16[512,256]{1,0:T(8,128)(2,1)S(1)}, u32[]{:S(2)}, u32[]{:S(2)}) collective-permute-start(bf16[512,256]{1,0:T(8,128)(2,1)} %refs_0_.1), channel_id=1, source_target_pairs={{0,1},{1,0},{2,3},{3,2},{4,5},{5,4},{6,7},{7,6},{8,9},{9,8},{10,11... | collective-permute-start | bytes 786440 | tf_op jit(solution)/shard_map/ppermute | solution.py:248
  3.7 1.6 %collective-permute-start = (bf16[512,256]{1,0:T(8,128)(2,1)}, bf16[512,256]{1,0:T(8,128)(2,1)S(1)}, u32[]{:S(2)}, u32[]{:S(2)}) collective-permute-start(bf16[512,256]{1,0:T(8,128)(2,1)} %refs_0_.1), channel_id=1, source_target_pairs={{0,4},{1,5},{2,6},{3,7},{4,8},{5,9},{6,10},{7,11},{8,12},{9,13},{1... | collective-permute-start | bytes 786440 | tf_op jit(solution)/shard_map/ppermute | solution.py:243
  5.3 1.5 %collective-permute-start.13 = (bf16[512,256]{1,0:T(8,128)(2,1)}, bf16[512,256]{1,0:T(8,128)(2,1)S(1)}, u32[]{:S(2)}, u32[]{:S(2)}) collective-permute-start(bf16[512,256]{1,0:T(8,128)(2,1)} %refs_0_.1), channel_id=1, source_target_pairs={{0,2},{1,3},{2,0},{3,1},{4,6},{5,7},{6,4},{7,5},{8,10},{9,11},{10,... | collective-permute-start | bytes 786440 | tf_op jit(solution)/shard_map/ppermute | solution.py:248
  6.8 2.2 %collective-permute-start.9 = (bf16[512,256]{1,0:T(8,128)(2,1)}, bf16[512,256]{1,0:T(8,128)(2,1)S(1)}, u32[]{:S(2)}, u32[]{:S(2)}) collective-permute-start(bf16[512,256]{1,0:T(8,128)(2,1)} %refs_0_.1), channel_id=1, source_target_pairs={{0,12},{1,13},{2,14},{3,15},{4,0},{5,1},{6,2},{7,3},{8,4},{9,5},{1... | collective-permute-start | bytes 786440 | tf_op jit(solution)/shard_map/ppermute | solution.py:243
  9.0 0.3 collective-permute-done.5.refs_1_
  9.3 3.4 %collective-permute-start.7 = (bf16[512,256]{1,0:T(8,128)(2,1)S(1)}, bf16[512,256]{1,0:T(8,128)(2,1)S(1)}, u32[]{:S(2)}, u32[]{:S(2)}) collective-permute-start(bf16[512,256]{1,0:T(8,128)(2,1)S(1)} %collective-permute-done.5.refs_1_), channel_id=1, source_target_pairs={{0,2},{1,3},{2,0},{3,1},{4,6},{5,7},{6,4},{7,5},{8,10},{9,11},{10,... | collective-permute-start | bytes 786440 | tf_op jit(solution)/shard_map/ppermute | solution.py:248
  12.7 2.2 %collective-permute-done.refs_4_ = bf16[512,256]{1,0:T(8,128)(2,1)S(1)} collective-permute-done((bf16[512,256]{1,0:T(8,128)(2,1)}, bf16[512,256]{1,0:T(8,128)(2,1)S(1)}, u32[]{:S(2)}, u32[]{:S(2)}) %collective-permute-start) | collective-permute-done | bytes 262176 | tf_op jit(solution)/shard_map/ppermute | solution.py:243
  14.9 0.0 collective-permute-start.1
  14.9 4.1 %prepare.1 = (bf16[4096,512]{1,0:T(8,128)(2,1)S(1)}, bf16[1024,512]{1,0:T(8,128)(2,1)S(1)}, bf16[1024,512]{1,0:T(8,128)(2,1)S(1)}) custom-call(s32[32]{0:T(128)} %cin.1, s32[4]{0:T(128)} %cout.1, s32[8,8]{1,0:T(8,128)} %allowed.1, s32[16]{0:T(128)} %slots.1, bf16[4096,512]{1,0:T(8,128)(2,1)} %layer.1, bf16[512,2048]{1,0:T(8,128)(2,1)} %projector.1), custom_call_target="tpu_custom_call" | custom-call | bytes 8388608 | tf_op jit(solution)/shard_map/prepare/pallas_call | solution.py:83
  19.0 0.1 collective-permute-start.17
  19.1 0.0 collective-permute-done.13.refs_2_
  19.1 3.1 %collective-permute-start.14 = (bf16[512,256]{1,0:T(8,128)(2,1)S(1)}, bf16[512,256]{1,0:T(8,128)(2,1)S(1)}, u32[]{:S(2)}, u32[]{:S(2)}) collective-permute-start(bf16[512,256]{1,0:T(8,128)(2,1)S(1)} %collective-permute-done.refs_4_), channel_id=1, source_target_pairs={{0,2},{1,3},{2,0},{3,1},{4,6},{5,7},{6,4},{7,5},{8,10},{9,11},{10,... | collective-permute-start | bytes 786440 | tf_op jit(solution)/shard_map/ppermute | solution.py:248
  22.2 0.0 collective-permute-done.9.refs_0_
  22.2 0.0 collective-permute-start.10
  22.2 0.0 collective-permute-done.7.refs_3_
  22.2 0.3 collective-permute-start.11
  22.5 2.3 %collective-permute-done.1.refs_0_ = bf16[512,256]{1,0:T(8,128)(2,1)S(1)} collective-permute-done((bf16[512,256]{1,0:T(8,128)(2,1)S(1)}, bf16[512,256]{1,0:T(8,128)(2,1)S(1)}, u32[]{:S(2)}, u32[]{:S(2)}) %collective-permute-start.1) | collective-permute-done | bytes 262176 | tf_op jit(solution)/shard_map/ppermute | solution.py:243
  24.8 3.3 %collective-permute-start.6 = (bf16[512,256]{1,0:T(8,128)(2,1)S(1)}, bf16[512,256]{1,0:T(8,128)(2,1)S(1)}, u32[]{:S(2)}, u32[]{:S(2)}) collective-permute-start(bf16[512,256]{1,0:T(8,128)(2,1)S(1)} %collective-permute-done.5.refs_1_), channel_id=1, source_target_pairs={{0,4},{1,5},{2,6},{3,7},{4,8},{5,9},{6,10},{7,11},{8,12},{9,13},{1... | collective-permute-start | bytes 786440 | tf_op jit(solution)/shard_map/ppermute | solution.py:243
  28.2 1.0 %collective-permute-done.14.refs_5_ = bf16[512,256]{1,0:T(8,128)(2,1)S(1)} collective-permute-done((bf16[512,256]{1,0:T(8,128)(2,1)S(1)}, bf16[512,256]{1,0:T(8,128)(2,1)S(1)}, u32[]{:S(2)}, u32[]{:S(2)}) %collective-permute-start.14) | collective-permute-done | bytes 262176 | tf_op jit(solution)/shard_map/ppermute | solution.py:248
  29.2 0.0 collective-permute-start.15
  29.2 1.5 %collective-permute-done.10.refs_1_ = bf16[512,256]{1,0:T(8,128)(2,1)S(1)} collective-permute-done((bf16[512,256]{1,0:T(8,128)(2,1)S(1)}, bf16[512,256]{1,0:T(8,128)(2,1)S(1)}, u32[]{:S(2)}, u32[]{:S(2)}) %collective-permute-start.10) | collective-permute-done | bytes 262176 | tf_op jit(solution)/shard_map/ppermute | solution.py:248
  30.6 0.8 %collective-permute-start.12 = (bf16[512,256]{1,0:T(8,128)(2,1)S(1)}, bf16[512,256]{1,0:T(8,128)(2,1)S(1)}, u32[]{:S(2)}, u32[]{:S(2)}) collective-permute-start(bf16[512,256]{1,0:T(8,128)(2,1)S(1)} %collective-permute-done.10.refs_1_), channel_id=1, source_target_pairs={{0,2},{1,3},{2,0},{3,1},{4,6},{5,7},{6,4},{7,5},{8,10},{9,11},{10,... | collective-permute-start | bytes 786440 | tf_op jit(solution)/shard_map/ppermute | solution.py:248
  31.5 1.3 %collective-permute-done.11.refs_2_ = bf16[512,256]{1,0:T(8,128)(2,1)S(1)} collective-permute-done((bf16[512,256]{1,0:T(8,128)(2,1)S(1)}, bf16[512,256]{1,0:T(8,128)(2,1)S(1)}, u32[]{:S(2)}, u32[]{:S(2)}) %collective-permute-start.11) | collective-permute-done | bytes 262176 | tf_op jit(solution)/shard_map/ppermute | solution.py:248
  32.8 1.7 %collective-permute-start.4 = (bf16[512,256]{1,0:T(8,128)(2,1)S(1)}, bf16[512,256]{1,0:T(8,128)(2,1)S(1)}, u32[]{:S(2)}, u32[]{:S(2)}) collective-permute-start(bf16[512,256]{1,0:T(8,128)(2,1)S(1)} %collective-permute-done.1.refs_0_), channel_id=1, source_target_pairs={{0,2},{1,3},{2,0},{3,1},{4,6},{5,7},{6,4},{7,5},{8,10},{9,11},{10,... | collective-permute-start | bytes 786440 | tf_op jit(solution)/shard_map/ppermute | solution.py:248
  34.5 0.0 collective-permute-done.6.refs_2_
  34.5 3.7 %collective-permute-start.8 = (bf16[512,256]{1,0:T(8,128)(2,1)S(1)}, bf16[512,256]{1,0:T(8,128)(2,1)S(1)}, u32[]{:S(2)}, u32[]{:S(2)}) collective-permute-start(bf16[512,256]{1,0:T(8,128)(2,1)S(1)} %collective-permute-done.7.refs_3_), channel_id=1, source_target_pairs={{0,4},{1,5},{2,6},{3,7},{4,8},{5,9},{6,10},{7,11},{8,12},{9,13},{1... | collective-permute-start | bytes 786440 | tf_op jit(solution)/shard_map/ppermute | solution.py:243
  38.2 0.0 collective-permute-done.15.refs_0_
  38.2 0.7 %collective-permute-start.2 = (bf16[256,256]{1,0:T(8,128)(2,1)S(1)}, bf16[256,256]{1,0:T(8,128)(2,1)S(1)}, u32[]{:S(2)}, u32[]{:S(2)}) collective-permute-start(bf16[256,256]{1,0:T(8,128)(2,1)S(1)} %get-tuple-element.13), channel_id=1, source_target_pairs={{0,1},{1,0},{2,3},{3,2},{4,5},{5,4},{6,7},{7,6},{8,9},{9,8},{10,11... | collective-permute-start | bytes 393224 | tf_op jit(solution)/shard_map/ppermute | solution.py:248
  38.9 4.3 %collective-permute-done.2.refs_0_ = bf16[256,256]{1,0:T(8,128)(2,1)S(1)} collective-permute-done((bf16[256,256]{1,0:T(8,128)(2,1)S(1)}, bf16[256,256]{1,0:T(8,128)(2,1)S(1)}, u32[]{:S(2)}, u32[]{:S(2)}) %collective-permute-start.2) | collective-permute-done | bytes 131104 | tf_op jit(solution)/shard_map/ppermute | solution.py:248
  43.2 1.2 %collective-permute-start.16 = (bf16[256,256]{1,0:T(8,128)(2,1)S(1)}, bf16[256,256]{1,0:T(8,128)(2,1)S(1)}, u32[]{:S(2)}, u32[]{:S(2)}) collective-permute-start(bf16[256,256]{1,0:T(8,128)(2,1)S(1)} %collective-permute-done.15.refs_0_), channel_id=1, source_target_pairs={{0,2},{1,3},{2,0},{3,1},{4,6},{5,7},{6,4},{7,5},{8,10},{9,11},{10,... | collective-permute-start | bytes 393224 | tf_op jit(solution)/shard_map/ppermute | solution.py:248
  44.4 0.9 %collective-permute-start.3 = (bf16[256,256]{1,0:T(8,128)(2,1)S(1)}, bf16[256,256]{1,0:T(8,128)(2,1)S(1)}, u32[]{:S(2)}, u32[]{:S(2)}) collective-permute-start(bf16[256,256]{1,0:T(8,128)(2,1)S(1)} %collective-permute-done.2.refs_0_), channel_id=1, source_target_pairs={{0,2},{1,3},{2,0},{3,1},{4,6},{5,7},{6,4},{7,5},{8,10},{9,11},{10,... | collective-permute-start | bytes 393224 | tf_op jit(solution)/shard_map/ppermute | solution.py:248
  45.2 1.0 %absorb.5.refs_4_ = f32[512,512]{1,0:T(8,128)S(1)} custom-call(bf16[4096,512]{1,0:T(8,128)(2,1)S(1)} %get-tuple-element.8.masked, bf16[512,256]{1,0:T(8,128)(2,1)S(1)} %copy-done, bf16[512,256]{1,0:T(8,128)(2,1)S(1)} %collective-permute-done.5.refs_1_, bf16[512,256]{1,0:T(8,128)(2,1)S(1)} %collective-permute-done.13.refs_2_, ...), custom_call_target="tpu_custom_call" | custom-call | flops 805306368 | bytes 3145728 | tf_op jit(solution)/shard_map/absorb/pallas_call | solution.py:124
  46.2 0.7 %absorb.6.refs_4_ = f32[512,512]{1,0:T(8,128)S(1)} custom-call(bf16[4096,512]{1,0:T(8,128)(2,1)S(1)} %get-tuple-element.8.masked, bf16[512,256]{1,0:T(8,128)(2,1)S(1)} %collective-permute-done.9.refs_0_, bf16[512,256]{1,0:T(8,128)(2,1)S(1)} %collective-permute-done.10.refs_1_, bf16[512,256]{1,0:T(8,128)(2,1)S(1)} %collective-permute-done.11.refs_2_, ...), custom_call_target="tpu_custom_call" | custom-call | flops 536870912 | bytes 2097152 | tf_op jit(solution)/shard_map/absorb/pallas_call | solution.py:124
  47.0 0.0 collective-permute-done.4.refs_1_
  47.0 0.0 collective-permute-done.8.refs_3_
  47.0 0.7 %absorb.7.refs_2_ = f32[512,512]{1,0:T(8,128)S(1)} custom-call(bf16[4096,512]{1,0:T(8,128)(2,1)S(1)} %get-tuple-element.8.masked, bf16[512,256]{1,0:T(8,128)(2,1)S(1)} %collective-permute-done.1.refs_0_, bf16[512,256]{1,0:T(8,128)(2,1)S(1)} %collective-permute-done.4.refs_1_, bf16[512,256]{1,0:T(8,128)(2,1)S(1)} %collective-permute-done.6.refs_2_, ...), custom_call_target="tpu_custom_call" | custom-call | flops 536870912 | bytes 2097152 | tf_op jit(solution)/shard_map/absorb/pallas_call | solution.py:124
  47.7 0.5 collective-permute-done.16.refs_1_
  48.2 0.3 absorb.9.contracted.refs_1_
  48.5 0.1 collective-permute-start.19
  48.6 1.0 %collective-permute-done.3.refs_1_ = bf16[256,256]{1,0:T(8,128)(2,1)S(1)} collective-permute-done((bf16[256,256]{1,0:T(8,128)(2,1)S(1)}, bf16[256,256]{1,0:T(8,128)(2,1)S(1)}, u32[]{:S(2)}, u32[]{:S(2)}) %collective-permute-start.3) | collective-permute-done | bytes 131104 | tf_op jit(solution)/shard_map/ppermute | solution.py:248
  49.6 0.3 absorb.8.contracted.refs_2_
  49.9 0.1 collective-permute-start.18
  50.0 0.4 corner_term.3.refs_0_
  50.4 0.8 %corner_term.4 = (f32[1024,512]{1,0:T(8,128)S(1)}, bf16[512,512]{1,0:T(8,128)(2,1)}) custom-call(bf16[1024,512]{1,0:T(8,128)(2,1)S(1)} %get-tuple-element.7.ordered, bf16[256,512]{1,0:T(8,128)(2,1)S(1)} %absorb.8.contracted.refs_2_, f32[1024,512]{1,0:T(8,128)S(1)} %corner_term.3.refs_0_, bf16[256,512]{1,0:T(8,128)(2,1)S(1)} %absorb.9.contracted.refs_1_, ...), custom_call_target="tpu_custom_call" | custom-call | flops 268435456 | bytes 262144 | tf_op jit(solution)/shard_map/corner_term/pallas_call | solution.py:159
  51.2 0.0 collective-permute-done.19.contracted
  51.3 0.0 collective-permute-done.17.ordered
  51.3 0.4 corner_term.5.total
  51.7 1.2 %corner.1 = bf16[1024,512]{1,0:T(8,128)(2,1)} custom-call(bf16[1024,512]{1,0:T(8,128)(2,1)S(1)} %collective-permute-done.17.ordered, bf16[256,512]{1,0:T(8,128)(2,1)S(1)} %collective-permute-done.18.contracted, f32[1024,512]{1,0:T(8,128)S(1)} %corner_term.5.total), custom_call_target="tpu_custom_call" | custom-call | flops 268435456 | bytes 1048576 | tf_op jit(solution)/shard_map/corner/pallas_call | solution.py:189
  (5 shorter events, 0.0 us)
Async XLA Ops:
  0.6 44.6 %copy-start = (bf16[512,256]{1,0:T(8,128)(2,1)S(1)}, bf16[512,256]{1,0:T(8,128)(2,1)}, u32[]{:S(2)}) copy-start(bf16[512,256]{1,0:T(8,128)(2,1)} %refs_0_.1) | copy-start | bytes 786436
  0.6 8.6 %collective-permute-start.5 = (bf16[512,256]{1,0:T(8,128)(2,1)}, bf16[512,256]{1,0:T(8,128)(2,1)S(1)}, u32[]{:S(2)}, u32[]{:S(2)}) collective-permute-start(bf16[512,256]{1,0:T(8,128)(2,1)} %refs_0_.1), channel_id=1, source_target_pairs={{0,1},{1,0},{2,3},{3,2},{4,5},{5,4},{6,7},{7,6},{8,9},{9,8},{10,11... | collective-permute-start | bytes 786440 | tf_op jit(solution)/shard_map/ppermute | solution.py:248
  3.7 11.2 %collective-permute-start = (bf16[512,256]{1,0:T(8,128)(2,1)}, bf16[512,256]{1,0:T(8,128)(2,1)S(1)}, u32[]{:S(2)}, u32[]{:S(2)}) collective-permute-start(bf16[512,256]{1,0:T(8,128)(2,1)} %refs_0_.1), channel_id=1, source_target_pairs={{0,4},{1,5},{2,6},{3,7},{4,8},{5,9},{6,10},{7,11},{8,12},{9,13},{1... | collective-permute-start | bytes 786440 | tf_op jit(solution)/shard_map/ppermute | solution.py:243
  5.3 13.9 %collective-permute-start.13 = (bf16[512,256]{1,0:T(8,128)(2,1)}, bf16[512,256]{1,0:T(8,128)(2,1)S(1)}, u32[]{:S(2)}, u32[]{:S(2)}) collective-permute-start(bf16[512,256]{1,0:T(8,128)(2,1)} %refs_0_.1), channel_id=1, source_target_pairs={{0,2},{1,3},{2,0},{3,1},{4,6},{5,7},{6,4},{7,5},{8,10},{9,11},{10,... | collective-permute-start | bytes 786440 | tf_op jit(solution)/shard_map/ppermute | solution.py:248
  6.8 15.4 %collective-permute-start.9 = (bf16[512,256]{1,0:T(8,128)(2,1)}, bf16[512,256]{1,0:T(8,128)(2,1)S(1)}, u32[]{:S(2)}, u32[]{:S(2)}) collective-permute-start(bf16[512,256]{1,0:T(8,128)(2,1)} %refs_0_.1), channel_id=1, source_target_pairs={{0,12},{1,13},{2,14},{3,15},{4,0},{5,1},{6,2},{7,3},{8,4},{9,5},{1... | collective-permute-start | bytes 786440 | tf_op jit(solution)/shard_map/ppermute | solution.py:243
  9.3 12.9 %collective-permute-start.7 = (bf16[512,256]{1,0:T(8,128)(2,1)S(1)}, bf16[512,256]{1,0:T(8,128)(2,1)S(1)}, u32[]{:S(2)}, u32[]{:S(2)}) collective-permute-start(bf16[512,256]{1,0:T(8,128)(2,1)S(1)} %collective-permute-done.5.refs_1_), channel_id=1, source_target_pairs={{0,2},{1,3},{2,0},{3,1},{4,6},{5,7},{6,4},{7,5},{8,10},{9,11},{10,... | collective-permute-start | bytes 786440 | tf_op jit(solution)/shard_map/ppermute | solution.py:248
  14.9 9.9 %collective-permute-start.1 = (bf16[512,256]{1,0:T(8,128)(2,1)S(1)}, bf16[512,256]{1,0:T(8,128)(2,1)S(1)}, u32[]{:S(2)}, u32[]{:S(2)}) collective-permute-start(bf16[512,256]{1,0:T(8,128)(2,1)S(1)} %collective-permute-done.refs_4_), channel_id=1, source_target_pairs={{0,4},{1,5},{2,6},{3,7},{4,8},{5,9},{6,10},{7,11},{8,12},{9,13},{1... | collective-permute-start | bytes 786440 | tf_op jit(solution)/shard_map/ppermute | solution.py:243
  19.0 32.2 %collective-permute-start.17 = (bf16[1024,512]{1,0:T(8,128)(2,1)S(1)}, bf16[1024,512]{1,0:T(8,128)(2,1)S(1)}, u32[]{:S(2)}, u32[]{:S(2)}) collective-permute-start(bf16[1024,512]{1,0:T(8,128)(2,1)S(1)} %get-tuple-element.10), channel_id=1, source_target_pairs={{0,16},{16,0},{1,17},{17,1},{2,18},{18,2},{3,19},{19,3},{4,20},{20... | collective-permute-start | bytes 3145736 | tf_op jit(solution)/shard_map/ppermute | solution.py:251
  19.1 10.0 %collective-permute-start.14 = (bf16[512,256]{1,0:T(8,128)(2,1)S(1)}, bf16[512,256]{1,0:T(8,128)(2,1)S(1)}, u32[]{:S(2)}, u32[]{:S(2)}) collective-permute-start(bf16[512,256]{1,0:T(8,128)(2,1)S(1)} %collective-permute-done.refs_4_), channel_id=1, source_target_pairs={{0,2},{1,3},{2,0},{3,1},{4,6},{5,7},{6,4},{7,5},{8,10},{9,11},{10,... | collective-permute-start | bytes 786440 | tf_op jit(solution)/shard_map/ppermute | solution.py:248
  22.2 8.4 %collective-permute-start.10 = (bf16[512,256]{1,0:T(8,128)(2,1)S(1)}, bf16[512,256]{1,0:T(8,128)(2,1)S(1)}, u32[]{:S(2)}, u32[]{:S(2)}) collective-permute-start(bf16[512,256]{1,0:T(8,128)(2,1)S(1)} %collective-permute-done.9.refs_0_), channel_id=1, source_target_pairs={{0,1},{1,0},{2,3},{3,2},{4,5},{5,4},{6,7},{7,6},{8,9},{9,8},{10,11... | collective-permute-start | bytes 786440 | tf_op jit(solution)/shard_map/ppermute | solution.py:248
  22.2 10.6 %collective-permute-start.11 = (bf16[512,256]{1,0:T(8,128)(2,1)S(1)}, bf16[512,256]{1,0:T(8,128)(2,1)S(1)}, u32[]{:S(2)}, u32[]{:S(2)}) collective-permute-start(bf16[512,256]{1,0:T(8,128)(2,1)S(1)} %collective-permute-done.9.refs_0_), channel_id=1, source_target_pairs={{0,2},{1,3},{2,0},{3,1},{4,6},{5,7},{6,4},{7,5},{8,10},{9,11},{10,... | collective-permute-start | bytes 786440 | tf_op jit(solution)/shard_map/ppermute | solution.py:248
  24.8 9.7 %collective-permute-start.6 = (bf16[512,256]{1,0:T(8,128)(2,1)S(1)}, bf16[512,256]{1,0:T(8,128)(2,1)S(1)}, u32[]{:S(2)}, u32[]{:S(2)}) collective-permute-start(bf16[512,256]{1,0:T(8,128)(2,1)S(1)} %collective-permute-done.5.refs_1_), channel_id=1, source_target_pairs={{0,4},{1,5},{2,6},{3,7},{4,8},{5,9},{6,10},{7,11},{8,12},{9,13},{1... | collective-permute-start | bytes 786440 | tf_op jit(solution)/shard_map/ppermute | solution.py:243
  29.2 9.1 %collective-permute-start.15 = (bf16[256,256]{1,0:T(8,128)(2,1)S(1)}, bf16[256,256]{1,0:T(8,128)(2,1)S(1)}, u32[]{:S(2)}, u32[]{:S(2)}) collective-permute-start(bf16[256,256]{1,0:T(8,128)(2,1)S(1)} %get-tuple-element.12), channel_id=1, source_target_pairs={{0,1},{1,0},{2,3},{3,2},{4,5},{5,4},{6,7},{7,6},{8,9},{9,8},{10,11... | collective-permute-start | bytes 393224 | tf_op jit(solution)/shard_map/ppermute | solution.py:248
  30.6 13.7 %collective-permute-start.12 = (bf16[512,256]{1,0:T(8,128)(2,1)S(1)}, bf16[512,256]{1,0:T(8,128)(2,1)S(1)}, u32[]{:S(2)}, u32[]{:S(2)}) collective-permute-start(bf16[512,256]{1,0:T(8,128)(2,1)S(1)} %collective-permute-done.10.refs_1_), channel_id=1, source_target_pairs={{0,2},{1,3},{2,0},{3,1},{4,6},{5,7},{6,4},{7,5},{8,10},{9,11},{10,... | collective-permute-start | bytes 786440 | tf_op jit(solution)/shard_map/ppermute | solution.py:248
  32.8 14.2 %collective-permute-start.4 = (bf16[512,256]{1,0:T(8,128)(2,1)S(1)}, bf16[512,256]{1,0:T(8,128)(2,1)S(1)}, u32[]{:S(2)}, u32[]{:S(2)}) collective-permute-start(bf16[512,256]{1,0:T(8,128)(2,1)S(1)} %collective-permute-done.1.refs_0_), channel_id=1, source_target_pairs={{0,2},{1,3},{2,0},{3,1},{4,6},{5,7},{6,4},{7,5},{8,10},{9,11},{10,... | collective-permute-start | bytes 786440 | tf_op jit(solution)/shard_map/ppermute | solution.py:248
  34.5 12.4 %collective-permute-start.8 = (bf16[512,256]{1,0:T(8,128)(2,1)S(1)}, bf16[512,256]{1,0:T(8,128)(2,1)S(1)}, u32[]{:S(2)}, u32[]{:S(2)}) collective-permute-start(bf16[512,256]{1,0:T(8,128)(2,1)S(1)} %collective-permute-done.7.refs_3_), channel_id=1, source_target_pairs={{0,4},{1,5},{2,6},{3,7},{4,8},{5,9},{6,10},{7,11},{8,12},{9,13},{1... | collective-permute-start | bytes 786440 | tf_op jit(solution)/shard_map/ppermute | solution.py:243
  38.2 5.0 %collective-permute-start.2 = (bf16[256,256]{1,0:T(8,128)(2,1)S(1)}, bf16[256,256]{1,0:T(8,128)(2,1)S(1)}, u32[]{:S(2)}, u32[]{:S(2)}) collective-permute-start(bf16[256,256]{1,0:T(8,128)(2,1)S(1)} %get-tuple-element.13), channel_id=1, source_target_pairs={{0,1},{1,0},{2,3},{3,2},{4,5},{5,4},{6,7},{7,6},{8,9},{9,8},{10,11... | collective-permute-start | bytes 393224 | tf_op jit(solution)/shard_map/ppermute | solution.py:248
  43.2 5.0 %collective-permute-start.16 = (bf16[256,256]{1,0:T(8,128)(2,1)S(1)}, bf16[256,256]{1,0:T(8,128)(2,1)S(1)}, u32[]{:S(2)}, u32[]{:S(2)}) collective-permute-start(bf16[256,256]{1,0:T(8,128)(2,1)S(1)} %collective-permute-done.15.refs_0_), channel_id=1, source_target_pairs={{0,2},{1,3},{2,0},{3,1},{4,6},{5,7},{6,4},{7,5},{8,10},{9,11},{10,... | collective-permute-start | bytes 393224 | tf_op jit(solution)/shard_map/ppermute | solution.py:248
  44.4 5.2 %collective-permute-start.3 = (bf16[256,256]{1,0:T(8,128)(2,1)S(1)}, bf16[256,256]{1,0:T(8,128)(2,1)S(1)}, u32[]{:S(2)}, u32[]{:S(2)}) collective-permute-start(bf16[256,256]{1,0:T(8,128)(2,1)S(1)} %collective-permute-done.2.refs_0_), channel_id=1, source_target_pairs={{0,2},{1,3},{2,0},{3,1},{4,6},{5,7},{6,4},{7,5},{8,10},{9,11},{10,... | collective-permute-start | bytes 393224 | tf_op jit(solution)/shard_map/ppermute | solution.py:248
  48.5 2.8 %collective-permute-start.19 = (bf16[256,512]{1,0:T(8,128)(2,1)S(1)}, bf16[256,512]{1,0:T(8,128)(2,1)S(1)}, u32[]{:S(2)}, u32[]{:S(2)}) collective-permute-start(bf16[256,512]{1,0:T(8,128)(2,1)S(1)} %absorb.9.contracted.refs_1_), channel_id=1, source_target_pairs={{0,16},{16,0},{1,17},{17,1},{2,18},{18,2},{3,19},{19,3},{4,20},{20... | collective-permute-start | bytes 786440 | tf_op jit(solution)/shard_map/ppermute | solution.py:251
  49.9 1.8 %collective-permute-start.18 = (bf16[256,512]{1,0:T(8,128)(2,1)S(1)}, bf16[256,512]{1,0:T(8,128)(2,1)S(1)}, u32[]{:S(2)}, u32[]{:S(2)}) collective-permute-start(bf16[256,512]{1,0:T(8,128)(2,1)S(1)} %absorb.8.contracted.refs_2_), channel_id=1, source_target_pairs={{0,16},{16,0},{1,17},{17,1},{2,18},{18,2},{3,19},{19,3},{4,20},{20... | collective-permute-start | bytes 786440 | tf_op jit(solution)/shard_map/ppermute | solution.py:251

commit v3 on v2

--- a/solution.py
+++ b/solution.py
@@ -111,10 +111,11 @@
     for slot, which in names:
         block = lax.rem(plane + (planes - slot), planes) * 4 + (spot ^ flips[which])
         layers.append(masked[pl.ds(pl.multiple_of(block * depth, depth), depth), :])
-    wide = jnp.concatenate([e[...] for e in edges], axis=1)
+    rows = out.shape[0]
+    wide = jnp.concatenate([e[...] if e.shape[0] == rows else e[at:at + rows, :] for e in edges], axis=1)
     total = jnp.dot(wide, jnp.concatenate(layers, axis=0), preferred_element_type=jnp.float32)
     if not fresh:
-        total = total + refs[count][at:at + wide.shape[0], :]
+        total = total + refs[count][at:at + rows, :]
     out[...] = total.astype(out.dtype)
 
 
@@ -201,30 +202,25 @@
 
 
 def plan(planes):
-    up = planes // 2
+    up, below = planes // 2, planes - 1
     whole = lambda s: tuple((s, kind) for kind in ("own", "first", "second", "both"))
+    hop = lambda s: [("hop", s + 1)] if s < up else [("hop", s - 1)] if s > up + 1 else []
     late = []
-    for s in range(1, up + 1):
-        late += [s] if s > 1 else []
-        late += [planes - s] if s < planes - s else []
-    steps = [("hop", 1), ("first", 0), ("second", 0), ("hop", planes - 1), ("prepare",)]
-    steps += [("both", 0), ("hop", 2), ("second", 1)]
-    for i, s in enumerate(late):
-        steps += [("first", s)]
-        hop = [("hop", s + 1 if s < up else s - 1)] if 1 < s < up or s > up + 1 else []
-        if i == 0:
-            steps += hop + [("pass",), ("relay", "first"), ("second", s)]
-            continue
-        if i == 1:
-            steps += [("absorb", 0, whole(0) + ((1, "own"), (1, "second")))]
-        else:
-            steps += [("absorb", late[i - 2], whole(late[i - 2]))]
-        steps += [("both", late[i - 1]), ("second", s)] + hop
-        if i == 1:
+    for s in range(2, up + 1):
+        late += [s] + ([planes - s] if s < planes - s else [])
+    steps = [("hop", 1), ("first", 0), ("second", 0), ("hop", below), ("prepare",)]
+    steps += [("both", 0), ("hop", 2), ("first", 1), ("second", 1), ("pass",)]
+    steps += hop(below) + [("second", below), ("relay", "first")]
+    for before, s in zip([1] + late, late):
+        steps += [("first", s), ("both", before)] + hop(s)
+        steps += [("second", s)]
+        if before == 1:
             steps += [("relay", "both")]
     last = late[-1]
-    steps += [("both", last)] + [("absorb", s, whole(s)) for s in late[-2:-1]]
-    return steps + [("absorb", last, ((last, "own"), (last, "second"), (1, "first"), (1, "both")))]
+    steps += [("both", last), ("absorb", 0, whole(0) + whole(1))]
+    steps += [("absorb", s, whole(s)) for s in late[:-1]]
+    rest = ((last, "own"), (last, "second"), (below, "own"), (below, "first"), (below, "second"))
+    return steps + [("absorb", last, rest)]
 
 
 def last_slot(planes):
@@ -269,7 +265,7 @@
         elif kind == "both":
             got[(kind, s)] = across(got[("first", s)], 2)
         elif kind == "relay":
-            got[(s, 1)] = plane_shift(got[(s, 0)], 1)
+            got[(s, planes - 1)] = plane_shift(got[(s, 0)], -1)
         elif kind == "prepare":
             tables = (charge_in, charge_out, allowed)
             masked, theirs = prepare(groups, tables, owner_slot_tile, double_layer, projector)
@@ -281,10 +277,10 @@
             blocks = [got[(which, slot)] for slot, which in names]
             total = absorb(planes, names, masked, blocks, total)
 
-    names = [(last, "first"), (last, "both")]
+    names = [(last, "first"), (last, "both"), (planes - 1, "both")]
     pieces, held, corner = [], [], None
     for i in range(PIECES):
-        blocks = [got[("firsts", i)], got[("boths", i)]]
+        blocks = [got[("firsts", i)], got[("boths", i)], got[("both", planes - 1)]]
         pieces.append(absorb(planes, names, masked, blocks, total, i * height, True))
         for k in range(1, groups):
             held.append((k, i * height, row_shift(pieces[i], k)))

time: 53.1 us -> 51 us (0.960)
  waiting for transfers between devices: 14.4 us -> 11.5 us
  starting transfers between devices: 27.7 us -> 28.6 us
    ppermute x12, waiting for transfers between devices: 9.81 us -> 4.25 us  [across(): return lax.ppermute(value, ('row', 'col'), pairs)]
    ppermute x5, starting transfers between devices: 10.9 us -> 14.6 us  [plane_shift(): lax.ppermute(value, 'col', [(c, (c // 4 + by) % planes * 4 + c % 4) for c...]
    ppermute x12, starting transfers between devices: 16.6 us -> 13.8 us  [across(): return lax.ppermute(value, ('row', 'col'), pairs)]
    ppermute x5, waiting for transfers between devices: 4.54 us -> 7.23 us  [plane_shift(): lax.ppermute(value, 'col', [(c, (c // 4 + by) % planes * 4 + c % 4) for c...]
    pallas_call x5 -> x4, Pallas kernels: 3.01 us -> 2.83 us  [absorb(): pl.pallas_call(functools.partial(absorb_body, planes, names, total is Non...]
  transfers between devices with their start and end apart: 20 -> 20, of which waited for: 9 -> 6; matrix products, arithmetic and copies ran while one was open for 0% -> 0% of each run, Pallas kernels for 17% -> 17%
where the time goes in v3:
time: 51 us; the launch traced here: 50.8 us
  starting transfers between devices  28.6 us (56%)
  waiting for transfers between devices  11.5 us (23%)
  Pallas kernels  9.9 us (19%)
  between operations  0.8 us (2%)
    ppermute x5, starting transfers between devices, plane_shift(): lax.ppermute(value, 'col', [(c, (c // 4 + by) % planes * 4 + c % 4) for c...  14.6 us
    ppermute x12, starting transfers between devices, across(): return lax.ppermute(value, ('row', 'col'), pairs)  13.8 us
    ppermute x5, waiting for transfers between devices, plane_shift(): lax.ppermute(value, 'col', [(c, (c // 4 + by) % planes * 4 + c % 4) for c...  7.23 us
    ppermute x12, waiting for transfers between devices, across(): return lax.ppermute(value, ('row', 'col'), pairs)  4.25 us
    pallas_call x1, Pallas kernels, prepare(): pl.pallas_call(functools.partial(prepare_body, groups, chunks), out_shape...  4.13 us
    pallas_call x4, Pallas kernels, absorb(): pl.pallas_call(functools.partial(absorb_body, planes, names, total is Non...  2.83 us
    pallas_call x3, Pallas kernels, corner_term(): pl.pallas_call(functools.partial(corner_term_body, start, total is None,...  1.71 us
    pallas_call x1, Pallas kernels, corner_sum(): pl.pallas_call(functools.partial(corner_body, start, chunks), out_shape=j...  1.23 us
  transfers between devices with their start and end apart: 20, of which 6 were waited for; matrix products, arithmetic and copies ran while one was open for 0% of the time, Pallas kernels for 17%

profile of v3, /device:TPU:0, one launch (start us, length us, event | category | flops | bytes accessed | tf_op | source)
XLA Modules:
  0.0 50.8 jit_solution(2682444765804888939)
XLA Ops:
  0.6 3.1 %collective-permute-start = (bf16[512,256]{1,0:T(8,128)(2,1)}, bf16[512,256]{1,0:T(8,128)(2,1)S(1)}, u32[]{:S(2)}, u32[]{:S(2)}) collective-permute-start(bf16[512,256]{1,0:T(8,128)(2,1)} %refs_0_.1), channel_id=1, source_target_pairs={{0,4},{1,5},{2,6},{3,7},{4,8},{5,9},{6,10},{7,11},{8,12},{9,13},{1... | collective-permute-start | bytes 786440 | tf_op jit(solution)/shard_map/ppermute | solution.py:239
  3.7 1.5 %collective-permute-start.4 = (bf16[512,256]{1,0:T(8,128)(2,1)}, bf16[512,256]{1,0:T(8,128)(2,1)S(1)}, u32[]{:S(2)}, u32[]{:S(2)}) collective-permute-start(bf16[512,256]{1,0:T(8,128)(2,1)} %refs_0_.1), channel_id=1, source_target_pairs={{0,1},{1,0},{2,3},{3,2},{4,5},{5,4},{6,7},{7,6},{8,9},{9,8},{10,11... | collective-permute-start | bytes 786440 | tf_op jit(solution)/shard_map/ppermute | solution.py:244
  5.2 1.5 %collective-permute-start.11 = (bf16[512,256]{1,0:T(8,128)(2,1)}, bf16[512,256]{1,0:T(8,128)(2,1)S(1)}, u32[]{:S(2)}, u32[]{:S(2)}) collective-permute-start(bf16[512,256]{1,0:T(8,128)(2,1)} %refs_0_.1), channel_id=1, source_target_pairs={{0,2},{1,3},{2,0},{3,1},{4,6},{5,7},{6,4},{7,5},{8,10},{9,11},{10,... | collective-permute-start | bytes 786440 | tf_op jit(solution)/shard_map/ppermute | solution.py:244
  6.8 2.2 %collective-permute-start.8 = (bf16[512,256]{1,0:T(8,128)(2,1)}, bf16[512,256]{1,0:T(8,128)(2,1)S(1)}, u32[]{:S(2)}, u32[]{:S(2)}) collective-permute-start(bf16[512,256]{1,0:T(8,128)(2,1)} %refs_0_.1), channel_id=1, source_target_pairs={{0,12},{1,13},{2,14},{3,15},{4,0},{5,1},{6,2},{7,3},{8,4},{9,5},{1... | collective-permute-start | bytes 786440 | tf_op jit(solution)/shard_map/ppermute | solution.py:239
  9.0 4.2 %collective-permute-done.refs_4_ = bf16[512,256]{1,0:T(8,128)(2,1)S(1)} collective-permute-done((bf16[512,256]{1,0:T(8,128)(2,1)}, bf16[512,256]{1,0:T(8,128)(2,1)S(1)}, u32[]{:S(2)}, u32[]{:S(2)}) %collective-permute-start) | collective-permute-done | bytes 262176 | tf_op jit(solution)/shard_map/ppermute | solution.py:239
  13.2 1.7 %collective-permute-start.12 = (bf16[512,256]{1,0:T(8,128)(2,1)S(1)}, bf16[512,256]{1,0:T(8,128)(2,1)S(1)}, u32[]{:S(2)}, u32[]{:S(2)}) collective-permute-start(bf16[512,256]{1,0:T(8,128)(2,1)S(1)} %collective-permute-done.refs_4_), channel_id=1, source_target_pairs={{0,1},{1,0},{2,3},{3,2},{4,5},{5,4},{6,7},{7,6},{8,9},{9,8},{10,11... | collective-permute-start | bytes 786440 | tf_op jit(solution)/shard_map/ppermute | solution.py:244
  14.9 1.5 %collective-permute-start.13 = (bf16[512,256]{1,0:T(8,128)(2,1)S(1)}, bf16[512,256]{1,0:T(8,128)(2,1)S(1)}, u32[]{:S(2)}, u32[]{:S(2)}) collective-permute-start(bf16[512,256]{1,0:T(8,128)(2,1)S(1)} %collective-permute-done.refs_4_), channel_id=1, source_target_pairs={{0,2},{1,3},{2,0},{3,1},{4,6},{5,7},{6,4},{7,5},{8,10},{9,11},{10,... | collective-permute-start | bytes 786440 | tf_op jit(solution)/shard_map/ppermute | solution.py:244
  16.4 0.0 collective-permute-done.4.refs_1_
  16.4 0.0 collective-permute-start.1
  16.4 4.1 %prepare.1 = (bf16[4096,512]{1,0:T(8,128)(2,1)S(1)}, bf16[1024,512]{1,0:T(8,128)(2,1)S(1)}, bf16[1024,512]{1,0:T(8,128)(2,1)S(1)}) custom-call(s32[32]{0:T(128)} %cin.1, s32[4]{0:T(128)} %cout.1, s32[8,8]{1,0:T(8,128)} %allowed.1, s32[16]{0:T(128)} %slots.1, bf16[4096,512]{1,0:T(8,128)(2,1)} %layer.1, bf16[512,2048]{1,0:T(8,128)(2,1)} %projector.1), custom_call_target="tpu_custom_call" | custom-call | bytes 8388608 | tf_op jit(solution)/shard_map/prepare/pallas_call | solution.py:83
  20.6 0.0 collective-permute-done.11.refs_2_
  20.6 0.1 collective-permute-start.17
  20.6 0.0 collective-permute-done.8.refs_2_
  20.7 1.1 %collective-permute-start.5 = (bf16[512,256]{1,0:T(8,128)(2,1)S(1)}, bf16[512,256]{1,0:T(8,128)(2,1)S(1)}, u32[]{:S(2)}, u32[]{:S(2)}) collective-permute-start(bf16[512,256]{1,0:T(8,128)(2,1)S(1)} %collective-permute-done.4.refs_1_), channel_id=1, source_target_pairs={{0,2},{1,3},{2,0},{3,1},{4,6},{5,7},{6,4},{7,5},{8,10},{9,11},{10,... | collective-permute-start | bytes 786440 | tf_op jit(solution)/shard_map/ppermute | solution.py:244
  21.7 0.0 collective-permute-done.12.refs_5_
  21.7 5.4 %collective-permute-start.9 = (bf16[512,256]{1,0:T(8,128)(2,1)S(1)}, bf16[512,256]{1,0:T(8,128)(2,1)S(1)}, u32[]{:S(2)}, u32[]{:S(2)}) collective-permute-start(bf16[512,256]{1,0:T(8,128)(2,1)S(1)} %collective-permute-done.4.refs_1_), channel_id=1, source_target_pairs={{0,12},{1,13},{2,14},{3,15},{4,0},{5,1},{6,2},{7,3},{8,4},{9,5},{1... | collective-permute-start | bytes 786440 | tf_op jit(solution)/shard_map/ppermute | solution.py:239
  27.1 0.0 collective-permute-done.13.refs_6_
  27.1 1.7 %collective-permute-start.10 = (bf16[512,256]{1,0:T(8,128)(2,1)S(1)}, bf16[512,256]{1,0:T(8,128)(2,1)S(1)}, u32[]{:S(2)}, u32[]{:S(2)}) collective-permute-start(bf16[512,256]{1,0:T(8,128)(2,1)S(1)} %collective-permute-done.8.refs_2_), channel_id=1, source_target_pairs={{0,2},{1,3},{2,0},{3,1},{4,6},{5,7},{6,4},{7,5},{8,10},{9,11},{10,... | collective-permute-start | bytes 786440 | tf_op jit(solution)/shard_map/ppermute | solution.py:244
  28.9 0.0 collective-permute-done.1.refs_0_
  28.9 0.3 collective-permute-start.14
  29.2 0.0 collective-permute-done.5.refs_3_
  29.2 0.9 %collective-permute-start.15 = (bf16[256,256]{1,0:T(8,128)(2,1)S(1)}, bf16[256,256]{1,0:T(8,128)(2,1)S(1)}, u32[]{:S(2)}, u32[]{:S(2)}) collective-permute-start(bf16[256,256]{1,0:T(8,128)(2,1)S(1)} %get-tuple-element.12), channel_id=1, source_target_pairs={{0,1},{1,0},{2,3},{3,2},{4,5},{5,4},{6,7},{7,6},{8,9},{9,8},{10,11... | collective-permute-start | bytes 393224 | tf_op jit(solution)/shard_map/ppermute | solution.py:244
  30.1 3.0 %collective-permute-done.9.refs_3_ = bf16[512,256]{1,0:T(8,128)(2,1)S(1)} collective-permute-done((bf16[512,256]{1,0:T(8,128)(2,1)S(1)}, bf16[512,256]{1,0:T(8,128)(2,1)S(1)}, u32[]{:S(2)}, u32[]{:S(2)}) %collective-permute-start.9) | collective-permute-done | bytes 262176 | tf_op jit(solution)/shard_map/ppermute | solution.py:239
  33.2 0.7 %collective-permute-start.7 = (bf16[512,256]{1,0:T(8,128)(2,1)S(1)}, bf16[512,256]{1,0:T(8,128)(2,1)S(1)}, u32[]{:S(2)}, u32[]{:S(2)}) collective-permute-start(bf16[512,256]{1,0:T(8,128)(2,1)S(1)} %collective-permute-done.1.refs_0_), channel_id=1, source_target_pairs={{0,2},{1,3},{2,0},{3,1},{4,6},{5,7},{6,4},{7,5},{8,10},{9,11},{10,... | collective-permute-start | bytes 786440 | tf_op jit(solution)/shard_map/ppermute | solution.py:244
  33.9 1.1 %collective-permute-done.10.refs_4_ = bf16[512,256]{1,0:T(8,128)(2,1)S(1)} collective-permute-done((bf16[512,256]{1,0:T(8,128)(2,1)S(1)}, bf16[512,256]{1,0:T(8,128)(2,1)S(1)}, u32[]{:S(2)}, u32[]{:S(2)}) %collective-permute-start.10) | collective-permute-done | bytes 262176 | tf_op jit(solution)/shard_map/ppermute | solution.py:244
  34.9 0.8 %collective-permute-start.2 = (bf16[256,256]{1,0:T(8,128)(2,1)S(1)}, bf16[256,256]{1,0:T(8,128)(2,1)S(1)}, u32[]{:S(2)}, u32[]{:S(2)}) collective-permute-start(bf16[256,256]{1,0:T(8,128)(2,1)S(1)} %get-tuple-element.13), channel_id=1, source_target_pairs={{0,1},{1,0},{2,3},{3,2},{4,5},{5,4},{6,7},{7,6},{8,9},{9,8},{10,11... | collective-permute-start | bytes 393224 | tf_op jit(solution)/shard_map/ppermute | solution.py:244
  35.8 0.0 collective-permute-done.15.refs_0_
  35.8 3.8 %collective-permute-start.6 = (bf16[512,256]{1,0:T(8,128)(2,1)S(1)}, bf16[512,256]{1,0:T(8,128)(2,1)S(1)}, u32[]{:S(2)}, u32[]{:S(2)}) collective-permute-start(bf16[512,256]{1,0:T(8,128)(2,1)S(1)} %collective-permute-done.5.refs_3_), channel_id=1, source_target_pairs={{0,12},{1,13},{2,14},{3,15},{4,0},{5,1},{6,2},{7,3},{8,4},{9,5},{1... | collective-permute-start | bytes 786440 | tf_op jit(solution)/shard_map/ppermute | solution.py:239
  39.6 1.4 %collective-permute-done.2.refs_0_ = bf16[256,256]{1,0:T(8,128)(2,1)S(1)} collective-permute-done((bf16[256,256]{1,0:T(8,128)(2,1)S(1)}, bf16[256,256]{1,0:T(8,128)(2,1)S(1)}, u32[]{:S(2)}, u32[]{:S(2)}) %collective-permute-start.2) | collective-permute-done | bytes 131104 | tf_op jit(solution)/shard_map/ppermute | solution.py:244
  41.0 0.7 %collective-permute-start.16 = (bf16[256,256]{1,0:T(8,128)(2,1)S(1)}, bf16[256,256]{1,0:T(8,128)(2,1)S(1)}, u32[]{:S(2)}, u32[]{:S(2)}) collective-permute-start(bf16[256,256]{1,0:T(8,128)(2,1)S(1)} %collective-permute-done.15.refs_0_), channel_id=1, source_target_pairs={{0,2},{1,3},{2,0},{3,1},{4,6},{5,7},{6,4},{7,5},{8,10},{9,11},{10,... | collective-permute-start | bytes 393224 | tf_op jit(solution)/shard_map/ppermute | solution.py:244
  41.7 0.0 collective-permute-done.14.refs_7_
  41.7 1.3 %collective-permute-start.3 = (bf16[256,256]{1,0:T(8,128)(2,1)S(1)}, bf16[256,256]{1,0:T(8,128)(2,1)S(1)}, u32[]{:S(2)}, u32[]{:S(2)}) collective-permute-start(bf16[256,256]{1,0:T(8,128)(2,1)S(1)} %collective-permute-done.2.refs_0_), channel_id=1, source_target_pairs={{0,2},{1,3},{2,0},{3,1},{4,6},{5,7},{6,4},{7,5},{8,10},{9,11},{10,... | collective-permute-start | bytes 393224 | tf_op jit(solution)/shard_map/ppermute | solution.py:244
  43.0 1.2 %absorb.4.refs_5_ = f32[512,512]{1,0:T(8,128)S(1)} custom-call(bf16[4096,512]{1,0:T(8,128)(2,1)S(1)} %get-tuple-element.8.masked, bf16[512,256]{1,0:T(8,128)(2,1)S(1)} %copy-done, bf16[512,256]{1,0:T(8,128)(2,1)S(1)} %collective-permute-done.4.refs_1_, bf16[512,256]{1,0:T(8,128)(2,1)S(1)} %collective-permute-done.11.refs_2_, ...), custom_call_target="tpu_custom_call" | custom-call | flops 1073741824 | bytes 4194304 | tf_op jit(solution)/shard_map/absorb/pallas_call | solution.py:125
  44.3 0.0 collective-permute-done.7.refs_1_
  44.3 0.9 %absorb.5.refs_3_ = f32[512,512]{1,0:T(8,128)S(1)} custom-call(bf16[4096,512]{1,0:T(8,128)(2,1)S(1)} %get-tuple-element.8.masked, bf16[512,256]{1,0:T(8,128)(2,1)S(1)} %collective-permute-done.1.refs_0_, bf16[512,256]{1,0:T(8,128)(2,1)S(1)} %collective-permute-done.7.refs_1_, bf16[512,256]{1,0:T(8,128)(2,1)S(1)} %collective-permute-done.8.refs_2_, ...), custom_call_target="tpu_custom_call" | custom-call | flops 671088640 | bytes 2621440 | tf_op jit(solution)/shard_map/absorb/pallas_call | solution.py:125
  45.1 0.0 collective-permute-done.6.refs_2_
  45.1 0.8 %collective-permute-done.16.refs_1_ = bf16[256,256]{1,0:T(8,128)(2,1)S(1)} collective-permute-done((bf16[256,256]{1,0:T(8,128)(2,1)S(1)}, bf16[256,256]{1,0:T(8,128)(2,1)S(1)}, u32[]{:S(2)}, u32[]{:S(2)}) %collective-permute-start.16) | collective-permute-done | bytes 131104 | tf_op jit(solution)/shard_map/ppermute | solution.py:244
  45.9 0.4 absorb.7.contracted.refs_1_
  46.3 0.1 collective-permute-start.19
  46.4 1.0 %collective-permute-done.3.refs_1_ = bf16[256,256]{1,0:T(8,128)(2,1)S(1)} collective-permute-done((bf16[256,256]{1,0:T(8,128)(2,1)S(1)}, bf16[256,256]{1,0:T(8,128)(2,1)S(1)}, u32[]{:S(2)}, u32[]{:S(2)}) %collective-permute-start.3) | collective-permute-done | bytes 131104 | tf_op jit(solution)/shard_map/ppermute | solution.py:244
  47.4 0.4 absorb.6.contracted.refs_2_
  47.7 0.1 collective-permute-start.18
  47.8 0.4 corner_term.3.refs_0_
  48.3 0.8 %corner_term.4 = (f32[1024,512]{1,0:T(8,128)S(1)}, bf16[512,512]{1,0:T(8,128)(2,1)}) custom-call(bf16[1024,512]{1,0:T(8,128)(2,1)S(1)} %get-tuple-element.7.ordered, bf16[256,512]{1,0:T(8,128)(2,1)S(1)} %absorb.6.contracted.refs_2_, f32[1024,512]{1,0:T(8,128)S(1)} %corner_term.3.refs_0_, bf16[256,512]{1,0:T(8,128)(2,1)S(1)} %absorb.7.contracted.refs_1_, ...), custom_call_target="tpu_custom_call" | custom-call | flops 268435456 | bytes 262144 | tf_op jit(solution)/shard_map/corner_term/pallas_call | solution.py:160
  49.1 0.0 collective-permute-done.19.contracted
  49.1 0.0 collective-permute-done.17.ordered
  49.1 0.4 corner_term.5.total
  49.6 1.2 %corner.1 = bf16[1024,512]{1,0:T(8,128)(2,1)} custom-call(bf16[1024,512]{1,0:T(8,128)(2,1)S(1)} %collective-permute-done.17.ordered, bf16[256,512]{1,0:T(8,128)(2,1)S(1)} %collective-permute-done.18.contracted, f32[1024,512]{1,0:T(8,128)S(1)} %corner_term.5.total), custom_call_target="tpu_custom_call" | custom-call | flops 268435456 | bytes 1048576 | tf_op jit(solution)/shard_map/corner/pallas_call | solution.py:190
  (4 shorter events, 0.0 us)
Async XLA Ops:
  0.6 42.4 %copy-start = (bf16[512,256]{1,0:T(8,128)(2,1)S(1)}, bf16[512,256]{1,0:T(8,128)(2,1)}, u32[]{:S(2)}) copy-start(bf16[512,256]{1,0:T(8,128)(2,1)} %refs_0_.1) | copy-start | bytes 786436
  0.6 12.5 %collective-permute-start = (bf16[512,256]{1,0:T(8,128)(2,1)}, bf16[512,256]{1,0:T(8,128)(2,1)S(1)}, u32[]{:S(2)}, u32[]{:S(2)}) collective-permute-start(bf16[512,256]{1,0:T(8,128)(2,1)} %refs_0_.1), channel_id=1, source_target_pairs={{0,4},{1,5},{2,6},{3,7},{4,8},{5,9},{6,10},{7,11},{8,12},{9,13},{1... | collective-permute-start | bytes 786440 | tf_op jit(solution)/shard_map/ppermute | solution.py:239
  3.7 12.7 %collective-permute-start.4 = (bf16[512,256]{1,0:T(8,128)(2,1)}, bf16[512,256]{1,0:T(8,128)(2,1)S(1)}, u32[]{:S(2)}, u32[]{:S(2)}) collective-permute-start(bf16[512,256]{1,0:T(8,128)(2,1)} %refs_0_.1), channel_id=1, source_target_pairs={{0,1},{1,0},{2,3},{3,2},{4,5},{5,4},{6,7},{7,6},{8,9},{9,8},{10,11... | collective-permute-start | bytes 786440 | tf_op jit(solution)/shard_map/ppermute | solution.py:244
  5.2 15.3 %collective-permute-start.11 = (bf16[512,256]{1,0:T(8,128)(2,1)}, bf16[512,256]{1,0:T(8,128)(2,1)S(1)}, u32[]{:S(2)}, u32[]{:S(2)}) collective-permute-start(bf16[512,256]{1,0:T(8,128)(2,1)} %refs_0_.1), channel_id=1, source_target_pairs={{0,2},{1,3},{2,0},{3,1},{4,6},{5,7},{6,4},{7,5},{8,10},{9,11},{10,... | collective-permute-start | bytes 786440 | tf_op jit(solution)/shard_map/ppermute | solution.py:244
  6.8 13.9 %collective-permute-start.8 = (bf16[512,256]{1,0:T(8,128)(2,1)}, bf16[512,256]{1,0:T(8,128)(2,1)S(1)}, u32[]{:S(2)}, u32[]{:S(2)}) collective-permute-start(bf16[512,256]{1,0:T(8,128)(2,1)} %refs_0_.1), channel_id=1, source_target_pairs={{0,12},{1,13},{2,14},{3,15},{4,0},{5,1},{6,2},{7,3},{8,4},{9,5},{1... | collective-permute-start | bytes 786440 | tf_op jit(solution)/shard_map/ppermute | solution.py:239
  13.2 8.5 %collective-permute-start.12 = (bf16[512,256]{1,0:T(8,128)(2,1)S(1)}, bf16[512,256]{1,0:T(8,128)(2,1)S(1)}, u32[]{:S(2)}, u32[]{:S(2)}) collective-permute-start(bf16[512,256]{1,0:T(8,128)(2,1)S(1)} %collective-permute-done.refs_4_), channel_id=1, source_target_pairs={{0,1},{1,0},{2,3},{3,2},{4,5},{5,4},{6,7},{7,6},{8,9},{9,8},{10,11... | collective-permute-start | bytes 786440 | tf_op jit(solution)/shard_map/ppermute | solution.py:244
  14.9 12.3 %collective-permute-start.13 = (bf16[512,256]{1,0:T(8,128)(2,1)S(1)}, bf16[512,256]{1,0:T(8,128)(2,1)S(1)}, u32[]{:S(2)}, u32[]{:S(2)}) collective-permute-start(bf16[512,256]{1,0:T(8,128)(2,1)S(1)} %collective-permute-done.refs_4_), channel_id=1, source_target_pairs={{0,2},{1,3},{2,0},{3,1},{4,6},{5,7},{6,4},{7,5},{8,10},{9,11},{10,... | collective-permute-start | bytes 786440 | tf_op jit(solution)/shard_map/ppermute | solution.py:244
  16.4 12.4 %collective-permute-start.1 = (bf16[512,256]{1,0:T(8,128)(2,1)S(1)}, bf16[512,256]{1,0:T(8,128)(2,1)S(1)}, u32[]{:S(2)}, u32[]{:S(2)}) collective-permute-start(bf16[512,256]{1,0:T(8,128)(2,1)S(1)} %collective-permute-done.refs_4_), channel_id=1, source_target_pairs={{0,4},{1,5},{2,6},{3,7},{4,8},{5,9},{6,10},{7,11},{8,12},{9,13},{1... | collective-permute-start | bytes 786440 | tf_op jit(solution)/shard_map/ppermute | solution.py:239
  20.6 28.5 %collective-permute-start.17 = (bf16[1024,512]{1,0:T(8,128)(2,1)S(1)}, bf16[1024,512]{1,0:T(8,128)(2,1)S(1)}, u32[]{:S(2)}, u32[]{:S(2)}) collective-permute-start(bf16[1024,512]{1,0:T(8,128)(2,1)S(1)} %get-tuple-element.10), channel_id=1, source_target_pairs={{0,16},{16,0},{1,17},{17,1},{2,18},{18,2},{3,19},{19,3},{4,20},{20... | collective-permute-start | bytes 3145736 | tf_op jit(solution)/shard_map/ppermute | solution.py:247
  20.7 8.5 %collective-permute-start.5 = (bf16[512,256]{1,0:T(8,128)(2,1)S(1)}, bf16[512,256]{1,0:T(8,128)(2,1)S(1)}, u32[]{:S(2)}, u32[]{:S(2)}) collective-permute-start(bf16[512,256]{1,0:T(8,128)(2,1)S(1)} %collective-permute-done.4.refs_1_), channel_id=1, source_target_pairs={{0,2},{1,3},{2,0},{3,1},{4,6},{5,7},{6,4},{7,5},{8,10},{9,11},{10,... | collective-permute-start | bytes 786440 | tf_op jit(solution)/shard_map/ppermute | solution.py:244
  21.7 11.4 %collective-permute-start.9 = (bf16[512,256]{1,0:T(8,128)(2,1)S(1)}, bf16[512,256]{1,0:T(8,128)(2,1)S(1)}, u32[]{:S(2)}, u32[]{:S(2)}) collective-permute-start(bf16[512,256]{1,0:T(8,128)(2,1)S(1)} %collective-permute-done.4.refs_1_), channel_id=1, source_target_pairs={{0,12},{1,13},{2,14},{3,15},{4,0},{5,1},{6,2},{7,3},{8,4},{9,5},{1... | collective-permute-start | bytes 786440 | tf_op jit(solution)/shard_map/ppermute | solution.py:239
  27.1 7.8 %collective-permute-start.10 = (bf16[512,256]{1,0:T(8,128)(2,1)S(1)}, bf16[512,256]{1,0:T(8,128)(2,1)S(1)}, u32[]{:S(2)}, u32[]{:S(2)}) collective-permute-start(bf16[512,256]{1,0:T(8,128)(2,1)S(1)} %collective-permute-done.8.refs_2_), channel_id=1, source_target_pairs={{0,2},{1,3},{2,0},{3,1},{4,6},{5,7},{6,4},{7,5},{8,10},{9,11},{10,... | collective-permute-start | bytes 786440 | tf_op jit(solution)/shard_map/ppermute | solution.py:244
  28.9 12.8 %collective-permute-start.14 = (bf16[512,256]{1,0:T(8,128)(2,1)S(1)}, bf16[512,256]{1,0:T(8,128)(2,1)S(1)}, u32[]{:S(2)}, u32[]{:S(2)}) collective-permute-start(bf16[512,256]{1,0:T(8,128)(2,1)S(1)} %collective-permute-done.12.refs_5_), channel_id=1, source_target_pairs={{0,2},{1,3},{2,0},{3,1},{4,6},{5,7},{6,4},{7,5},{8,10},{9,11},{10,... | collective-permute-start | bytes 786440 | tf_op jit(solution)/shard_map/ppermute | solution.py:244
  29.2 6.6 %collective-permute-start.15 = (bf16[256,256]{1,0:T(8,128)(2,1)S(1)}, bf16[256,256]{1,0:T(8,128)(2,1)S(1)}, u32[]{:S(2)}, u32[]{:S(2)}) collective-permute-start(bf16[256,256]{1,0:T(8,128)(2,1)S(1)} %get-tuple-element.12), channel_id=1, source_target_pairs={{0,1},{1,0},{2,3},{3,2},{4,5},{5,4},{6,7},{7,6},{8,9},{9,8},{10,11... | collective-permute-start | bytes 393224 | tf_op jit(solution)/shard_map/ppermute | solution.py:244
  33.2 11.1 %collective-permute-start.7 = (bf16[512,256]{1,0:T(8,128)(2,1)S(1)}, bf16[512,256]{1,0:T(8,128)(2,1)S(1)}, u32[]{:S(2)}, u32[]{:S(2)}) collective-permute-start(bf16[512,256]{1,0:T(8,128)(2,1)S(1)} %collective-permute-done.1.refs_0_), channel_id=1, source_target_pairs={{0,2},{1,3},{2,0},{3,1},{4,6},{5,7},{6,4},{7,5},{8,10},{9,11},{10,... | collective-permute-start | bytes 786440 | tf_op jit(solution)/shard_map/ppermute | solution.py:244
  34.9 6.1 %collective-permute-start.2 = (bf16[256,256]{1,0:T(8,128)(2,1)S(1)}, bf16[256,256]{1,0:T(8,128)(2,1)S(1)}, u32[]{:S(2)}, u32[]{:S(2)}) collective-permute-start(bf16[256,256]{1,0:T(8,128)(2,1)S(1)} %get-tuple-element.13), channel_id=1, source_target_pairs={{0,1},{1,0},{2,3},{3,2},{4,5},{5,4},{6,7},{7,6},{8,9},{9,8},{10,11... | collective-permute-start | bytes 393224 | tf_op jit(solution)/shard_map/ppermute | solution.py:244
  35.8 9.4 %collective-permute-start.6 = (bf16[512,256]{1,0:T(8,128)(2,1)S(1)}, bf16[512,256]{1,0:T(8,128)(2,1)S(1)}, u32[]{:S(2)}, u32[]{:S(2)}) collective-permute-start(bf16[512,256]{1,0:T(8,128)(2,1)S(1)} %collective-permute-done.5.refs_3_), channel_id=1, source_target_pairs={{0,12},{1,13},{2,14},{3,15},{4,0},{5,1},{6,2},{7,3},{8,4},{9,5},{1... | collective-permute-start | bytes 786440 | tf_op jit(solution)/shard_map/ppermute | solution.py:239
  41.0 5.0 %collective-permute-start.16 = (bf16[256,256]{1,0:T(8,128)(2,1)S(1)}, bf16[256,256]{1,0:T(8,128)(2,1)S(1)}, u32[]{:S(2)}, u32[]{:S(2)}) collective-permute-start(bf16[256,256]{1,0:T(8,128)(2,1)S(1)} %collective-permute-done.15.refs_0_), channel_id=1, source_target_pairs={{0,2},{1,3},{2,0},{3,1},{4,6},{5,7},{6,4},{7,5},{8,10},{9,11},{10,... | collective-permute-start | bytes 393224 | tf_op jit(solution)/shard_map/ppermute | solution.py:244
  41.7 5.7 %collective-permute-start.3 = (bf16[256,256]{1,0:T(8,128)(2,1)S(1)}, bf16[256,256]{1,0:T(8,128)(2,1)S(1)}, u32[]{:S(2)}, u32[]{:S(2)}) collective-permute-start(bf16[256,256]{1,0:T(8,128)(2,1)S(1)} %collective-permute-done.2.refs_0_), channel_id=1, source_target_pairs={{0,2},{1,3},{2,0},{3,1},{4,6},{5,7},{6,4},{7,5},{8,10},{9,11},{10,... | collective-permute-start | bytes 393224 | tf_op jit(solution)/shard_map/ppermute | solution.py:244
  46.3 2.8 %collective-permute-start.19 = (bf16[256,512]{1,0:T(8,128)(2,1)S(1)}, bf16[256,512]{1,0:T(8,128)(2,1)S(1)}, u32[]{:S(2)}, u32[]{:S(2)}) collective-permute-start(bf16[256,512]{1,0:T(8,128)(2,1)S(1)} %absorb.7.contracted.refs_1_), channel_id=1, source_target_pairs={{0,16},{16,0},{1,17},{17,1},{2,18},{18,2},{3,19},{19,3},{4,20},{20... | collective-permute-start | bytes 786440 | tf_op jit(solution)/shard_map/ppermute | solution.py:247
  47.7 1.8 %collective-permute-start.18 = (bf16[256,512]{1,0:T(8,128)(2,1)S(1)}, bf16[256,512]{1,0:T(8,128)(2,1)S(1)}, u32[]{:S(2)}, u32[]{:S(2)}) collective-permute-start(bf16[256,512]{1,0:T(8,128)(2,1)S(1)} %absorb.6.contracted.refs_2_), channel_id=1, source_target_pairs={{0,16},{16,0},{1,17},{17,1},{2,18},{18,2},{3,19},{19,3},{4,20},{20... | collective-permute-start | bytes 786440 | tf_op jit(solution)/shard_map/ppermute | solution.py:247
